TPU v7x, 128 devices: a whole 4x4x4 slice. The times are simulated.
128 devices in a mesh: rack: 4 (over x_hi, core), node: 32 (over y, x_lo, z).
Axes of the slice: x: 4 (x_hi: 2, x_lo: 2; x = x_hi * 2 + x_lo), y: 4, z: 4, core: 2. Of those that a mesh axis runs over, the one named last changes fastest.
Arguments:
- stored: bfloat16 [2560, 8, 4096], P(('rack', 'node')), may hold values from -6 to 6
- coefficients: bfloat16 [256, 10, 8, 8], replicated, may hold values from -0.3 to 0.61
- helper_rack: int32 [256, 10], replicated, may hold values from 0 to 3, as said below
- helper_node: int32 [256, 10], replicated, may hold values from 0 to 31, as said below
- helper_block: int32 [256, 10], replicated, may hold values from 0 to 19, as said below
Outputs:
- rebuilt: float32 [256, 8, 4096], P(('rack', 'node'))
Inputs may be any that keep to these rules, and one draw needn't show every extreme that they name: Repair r is rebuilt on device r // 2, counted rack-major. Its 10 helpers are distinct devices other than that one. With devices counted rack-major as helper_rack * 32 + helper_node, (helper device minus owner device) mod (128) depends only on h and r mod 2. `helper_node`: follows the same rule as helper_rack. `helper_block`: each of a device's 20 stored blocks is read by exactly one pair of repair and helper.
All inputs are finite; a program needn't handle non-finite values.
Results may differ from a plain program's by a relative error of at most 0.0003.
Values sent between devices are 32-bit elements; how exact they have to be, the bound alone decides.
No kernel may reach another device: no remote copies, remote signals or barrier semaphores. Data moves between devices by JAX's collectives and lax.ppermute only.
A program may use at most 64 MiB of HBM per device.

v0:
```python
import jax
import jax.numpy as jnp
from jax import lax
from jax.sharding import PartitionSpec as P

HELPERS = 10
REP_DEV = 2


def from_behind(value, axis, steps):
    count = lax.axis_size(axis)
    pairs = [(source, (source + steps) % count) for source in range(count)]
    return lax.ppermute(value, axis, pairs)


def rotate(payload, moves):
    device_count = lax.axis_size(("rack", "node"))
    current = payload
    for section_bit in range((device_count - 1).bit_length()):
        arrived = from_behind(current, ("rack", "node"), 1 << section_bit)
        chosen = moves >> section_bit & 1 == 1
        current = jnp.where(chosen[:, None, None], arrived, current)
    return current


def on_device(stored, coefficients, helper_rack, helper_node, helper_block):
    node_count = lax.axis_size("node")
    device_count = lax.axis_size(("rack", "node"))
    my_device = lax.axis_index("rack") * node_count + lax.axis_index("node")
    offsets = (helper_rack[:REP_DEV] * node_count + helper_node[:REP_DEV]) % device_count
    owner = (my_device - offsets) % device_count
    position = jnp.arange(REP_DEV, dtype=jnp.int32)[:, None]
    repair_rows = owner * REP_DEV + position
    helper_slot = jnp.arange(HELPERS, dtype=jnp.int32)[None, :]
    local_rows = helper_block[repair_rows, helper_slot]
    coeffs_used = coefficients[repair_rows, helper_slot]
    blocks_used = stored[local_rows]
    contrib = jnp.einsum(
        "shpq,shql->shpl", coeffs_used, blocks_used, preferred_element_type=jnp.float32
    )
    next_offset = jnp.concatenate([offsets[:, 1:], jnp.zeros_like(offsets[:, :1])], 1)
    hop_moves = jnp.transpose((next_offset - offsets) % device_count)
    contrib_hops = jnp.transpose(contrib, (1, 0, 2, 3))

    def advance(partial_value, hop_data):
        term, moves = hop_data
        return (rotate(partial_value + term, moves), None)

    start_sum = jnp.zeros((REP_DEV,) + contrib.shape[2:], jnp.float32)
    rebuilt, unused = lax.scan(advance, start_sum, (contrib_hops, hop_moves))
    return rebuilt


def solution(mesh):
    placed = (P(("rack", "node"), None, None), P(), P(), P(), P())
    return jax.shard_map(
        on_device,
        mesh=mesh,
        in_specs=placed,
        out_specs=P(("rack", "node"), None, None),
        check_vma=False,
    )
```

profile of v0, /device:TPU:1, one launch (start us, length us, event | category | flops | bytes accessed | tf_op | source)
XLA Modules:
  0.0 733.9 jit_solution(13149024952125183431)
XLA Ops:
  14.0 719.2 %while.11 = (s32[]{:T(128)}, f32[2,8,4096]{2,1,0:T(8,128)S(1)}, s32[10,2]{1,0:T(8,128)S(1)}, f32[10,2,8,4096]{3,2,0,1:T(8,128)}, s32[]{:T(128)}, /*index=5*/s32[]{:T(128)}) while((s32[]{:T(128)}, f32[2,8,4096]{2,1,0:T(8,128)S(1)}, s32[10,2]{1,0:T(8,128)S(1)}, f32[10,2,8,4096]{3,2,0,1:T(8,128)}, s32[]{:T(128)}, ...), condition=%wide.region_1.2_spmd.clone, body=%wide.region_0.1_spmd.clone.sunk | while | flops 589869 | bytes 13631907 | solution.py:50
  17.5 12.9 %collective-permute-done = f32[2,8,4096]{2,1,0:T(8,128)S(1)} collective-permute-done((f32[2,8,4096]{2,1,0:T(8,128)S(1)}, f32[2,8,4096]{2,1,0:T(8,128)S(1)}, u32[]{:S(2)}, u32[]{:S(2)}) %collective-permute-start) | collective-permute-done | bytes 262176 | tf_op jit(solution)/shard_map/while/body/eval_jaxpr/ppermute | solution.py:13
  30.6 12.8 %collective-permute-done.1 = f32[2,8,4096]{2,1,0:T(8,128)S(1)} collective-permute-done((f32[2,8,4096]{2,1,0:T(8,128)S(1)}, f32[2,8,4096]{2,1,0:T(8,128)S(1)}, u32[]{:S(2)}, u32[]{:S(2)}) %collective-permute-start.1) | collective-permute-done | bytes 262176 | tf_op jit(solution)/shard_map/while/body/eval_jaxpr/ppermute | solution.py:13
  87.0 10.0 %collective-permute-done = f32[2,8,4096]{2,1,0:T(8,128)S(1)} collective-permute-done((f32[2,8,4096]{2,1,0:T(8,128)S(1)}, f32[2,8,4096]{2,1,0:T(8,128)S(1)}, u32[]{:S(2)}, u32[]{:S(2)}) %collective-permute-start) | collective-permute-done | bytes 262176 | tf_op jit(solution)/shard_map/while/body/eval_jaxpr/ppermute | solution.py:13
  97.2 10.3 %collective-permute-done.1 = f32[2,8,4096]{2,1,0:T(8,128)S(1)} collective-permute-done((f32[2,8,4096]{2,1,0:T(8,128)S(1)}, f32[2,8,4096]{2,1,0:T(8,128)S(1)}, u32[]{:S(2)}, u32[]{:S(2)}) %collective-permute-start.1) | collective-permute-done | bytes 262176 | tf_op jit(solution)/shard_map/while/body/eval_jaxpr/ppermute | solution.py:13
  115.7 9.8 %collective-permute-done.3 = f32[2,8,4096]{2,1,0:T(8,128)S(1)} collective-permute-done((f32[2,8,4096]{2,1,0:T(8,128)S(1)}, f32[2,8,4096]{2,1,0:T(8,128)S(1)}, u32[]{:S(2)}, u32[]{:S(2)}) %collective-permute-start.3) | collective-permute-done | bytes 262176 | tf_op jit(solution)/shard_map/while/body/eval_jaxpr/ppermute | solution.py:13
  125.7 9.6 %collective-permute-done.4 = f32[2,8,4096]{2,1,0:T(8,128)S(1)} collective-permute-done((f32[2,8,4096]{2,1,0:T(8,128)S(1)}, f32[2,8,4096]{2,1,0:T(8,128)S(1)}, u32[]{:S(2)}, u32[]{:S(2)}) %collective-permute-start.4) | collective-permute-done | bytes 262176 | tf_op jit(solution)/shard_map/while/body/eval_jaxpr/ppermute | solution.py:13
  135.4 10.4 %collective-permute-start.5 = (f32[2,8,4096]{2,1,0:T(8,128)S(1)}, f32[2,8,4096]{2,1,0:T(8,128)S(1)}, u32[]{:S(2)}, u32[]{:S(2)}) collective-permute-start(f32[2,8,4096]{2,1,0:T(8,128)S(1)} %broadcast_select_fusion.18), channel_id=1, source_target_pairs={{0,32},{1,33},{2,34},{3,35},{4,36},{5,37},{6,38},{7,39},{8,40},{9,... | collective-permute-start | bytes 786440 | tf_op jit(solution)/shard_map/while/body/eval_jaxpr/ppermute | solution.py:13
  158.9 10.0 %collective-permute-done = f32[2,8,4096]{2,1,0:T(8,128)S(1)} collective-permute-done((f32[2,8,4096]{2,1,0:T(8,128)S(1)}, f32[2,8,4096]{2,1,0:T(8,128)S(1)}, u32[]{:S(2)}, u32[]{:S(2)}) %collective-permute-start) | collective-permute-done | bytes 262176 | tf_op jit(solution)/shard_map/while/body/eval_jaxpr/ppermute | solution.py:13
  169.1 10.3 %collective-permute-done.1 = f32[2,8,4096]{2,1,0:T(8,128)S(1)} collective-permute-done((f32[2,8,4096]{2,1,0:T(8,128)S(1)}, f32[2,8,4096]{2,1,0:T(8,128)S(1)}, u32[]{:S(2)}, u32[]{:S(2)}) %collective-permute-start.1) | collective-permute-done | bytes 262176 | tf_op jit(solution)/shard_map/while/body/eval_jaxpr/ppermute | solution.py:13
  187.6 9.8 %collective-permute-done.3 = f32[2,8,4096]{2,1,0:T(8,128)S(1)} collective-permute-done((f32[2,8,4096]{2,1,0:T(8,128)S(1)}, f32[2,8,4096]{2,1,0:T(8,128)S(1)}, u32[]{:S(2)}, u32[]{:S(2)}) %collective-permute-start.3) | collective-permute-done | bytes 262176 | tf_op jit(solution)/shard_map/while/body/eval_jaxpr/ppermute | solution.py:13
  197.6 9.6 %collective-permute-done.4 = f32[2,8,4096]{2,1,0:T(8,128)S(1)} collective-permute-done((f32[2,8,4096]{2,1,0:T(8,128)S(1)}, f32[2,8,4096]{2,1,0:T(8,128)S(1)}, u32[]{:S(2)}, u32[]{:S(2)}) %collective-permute-start.4) | collective-permute-done | bytes 262176 | tf_op jit(solution)/shard_map/while/body/eval_jaxpr/ppermute | solution.py:13
  207.3 10.4 %collective-permute-start.5 = (f32[2,8,4096]{2,1,0:T(8,128)S(1)}, f32[2,8,4096]{2,1,0:T(8,128)S(1)}, u32[]{:S(2)}, u32[]{:S(2)}) collective-permute-start(f32[2,8,4096]{2,1,0:T(8,128)S(1)} %broadcast_select_fusion.18), channel_id=1, source_target_pairs={{0,32},{1,33},{2,34},{3,35},{4,36},{5,37},{6,38},{7,39},{8,40},{9,... | collective-permute-start | bytes 786440 | tf_op jit(solution)/shard_map/while/body/eval_jaxpr/ppermute | solution.py:13
  230.9 10.0 %collective-permute-done = f32[2,8,4096]{2,1,0:T(8,128)S(1)} collective-permute-done((f32[2,8,4096]{2,1,0:T(8,128)S(1)}, f32[2,8,4096]{2,1,0:T(8,128)S(1)}, u32[]{:S(2)}, u32[]{:S(2)}) %collective-permute-start) | collective-permute-done | bytes 262176 | tf_op jit(solution)/shard_map/while/body/eval_jaxpr/ppermute | solution.py:13
  241.0 10.3 %collective-permute-done.1 = f32[2,8,4096]{2,1,0:T(8,128)S(1)} collective-permute-done((f32[2,8,4096]{2,1,0:T(8,128)S(1)}, f32[2,8,4096]{2,1,0:T(8,128)S(1)}, u32[]{:S(2)}, u32[]{:S(2)}) %collective-permute-start.1) | collective-permute-done | bytes 262176 | tf_op jit(solution)/shard_map/while/body/eval_jaxpr/ppermute | solution.py:13
  259.6 9.8 %collective-permute-done.3 = f32[2,8,4096]{2,1,0:T(8,128)S(1)} collective-permute-done((f32[2,8,4096]{2,1,0:T(8,128)S(1)}, f32[2,8,4096]{2,1,0:T(8,128)S(1)}, u32[]{:S(2)}, u32[]{:S(2)}) %collective-permute-start.3) | collective-permute-done | bytes 262176 | tf_op jit(solution)/shard_map/while/body/eval_jaxpr/ppermute | solution.py:13
  269.6 9.6 %collective-permute-done.4 = f32[2,8,4096]{2,1,0:T(8,128)S(1)} collective-permute-done((f32[2,8,4096]{2,1,0:T(8,128)S(1)}, f32[2,8,4096]{2,1,0:T(8,128)S(1)}, u32[]{:S(2)}, u32[]{:S(2)}) %collective-permute-start.4) | collective-permute-done | bytes 262176 | tf_op jit(solution)/shard_map/while/body/eval_jaxpr/ppermute | solution.py:13
  279.2 10.4 %collective-permute-start.5 = (f32[2,8,4096]{2,1,0:T(8,128)S(1)}, f32[2,8,4096]{2,1,0:T(8,128)S(1)}, u32[]{:S(2)}, u32[]{:S(2)}) collective-permute-start(f32[2,8,4096]{2,1,0:T(8,128)S(1)} %broadcast_select_fusion.18), channel_id=1, source_target_pairs={{0,32},{1,33},{2,34},{3,35},{4,36},{5,37},{6,38},{7,39},{8,40},{9,... | collective-permute-start | bytes 786440 | tf_op jit(solution)/shard_map/while/body/eval_jaxpr/ppermute | solution.py:13
  302.8 10.0 %collective-permute-done = f32[2,8,4096]{2,1,0:T(8,128)S(1)} collective-permute-done((f32[2,8,4096]{2,1,0:T(8,128)S(1)}, f32[2,8,4096]{2,1,0:T(8,128)S(1)}, u32[]{:S(2)}, u32[]{:S(2)}) %collective-permute-start) | collective-permute-done | bytes 262176 | tf_op jit(solution)/shard_map/while/body/eval_jaxpr/ppermute | solution.py:13
  312.9 10.3 %collective-permute-done.1 = f32[2,8,4096]{2,1,0:T(8,128)S(1)} collective-permute-done((f32[2,8,4096]{2,1,0:T(8,128)S(1)}, f32[2,8,4096]{2,1,0:T(8,128)S(1)}, u32[]{:S(2)}, u32[]{:S(2)}) %collective-permute-start.1) | collective-permute-done | bytes 262176 | tf_op jit(solution)/shard_map/while/body/eval_jaxpr/ppermute | solution.py:13
  331.5 9.8 %collective-permute-done.3 = f32[2,8,4096]{2,1,0:T(8,128)S(1)} collective-permute-done((f32[2,8,4096]{2,1,0:T(8,128)S(1)}, f32[2,8,4096]{2,1,0:T(8,128)S(1)}, u32[]{:S(2)}, u32[]{:S(2)}) %collective-permute-start.3) | collective-permute-done | bytes 262176 | tf_op jit(solution)/shard_map/while/body/eval_jaxpr/ppermute | solution.py:13
  341.5 9.6 %collective-permute-done.4 = f32[2,8,4096]{2,1,0:T(8,128)S(1)} collective-permute-done((f32[2,8,4096]{2,1,0:T(8,128)S(1)}, f32[2,8,4096]{2,1,0:T(8,128)S(1)}, u32[]{:S(2)}, u32[]{:S(2)}) %collective-permute-start.4) | collective-permute-done | bytes 262176 | tf_op jit(solution)/shard_map/while/body/eval_jaxpr/ppermute | solution.py:13
  351.2 10.4 %collective-permute-start.5 = (f32[2,8,4096]{2,1,0:T(8,128)S(1)}, f32[2,8,4096]{2,1,0:T(8,128)S(1)}, u32[]{:S(2)}, u32[]{:S(2)}) collective-permute-start(f32[2,8,4096]{2,1,0:T(8,128)S(1)} %broadcast_select_fusion.18), channel_id=1, source_target_pairs={{0,32},{1,33},{2,34},{3,35},{4,36},{5,37},{6,38},{7,39},{8,40},{9,... | collective-permute-start | bytes 786440 | tf_op jit(solution)/shard_map/while/body/eval_jaxpr/ppermute | solution.py:13
  374.7 10.0 %collective-permute-done = f32[2,8,4096]{2,1,0:T(8,128)S(1)} collective-permute-done((f32[2,8,4096]{2,1,0:T(8,128)S(1)}, f32[2,8,4096]{2,1,0:T(8,128)S(1)}, u32[]{:S(2)}, u32[]{:S(2)}) %collective-permute-start) | collective-permute-done | bytes 262176 | tf_op jit(solution)/shard_map/while/body/eval_jaxpr/ppermute | solution.py:13
  384.9 10.3 %collective-permute-done.1 = f32[2,8,4096]{2,1,0:T(8,128)S(1)} collective-permute-done((f32[2,8,4096]{2,1,0:T(8,128)S(1)}, f32[2,8,4096]{2,1,0:T(8,128)S(1)}, u32[]{:S(2)}, u32[]{:S(2)}) %collective-permute-start.1) | collective-permute-done | bytes 262176 | tf_op jit(solution)/shard_map/while/body/eval_jaxpr/ppermute | solution.py:13
  403.4 9.8 %collective-permute-done.3 = f32[2,8,4096]{2,1,0:T(8,128)S(1)} collective-permute-done((f32[2,8,4096]{2,1,0:T(8,128)S(1)}, f32[2,8,4096]{2,1,0:T(8,128)S(1)}, u32[]{:S(2)}, u32[]{:S(2)}) %collective-permute-start.3) | collective-permute-done | bytes 262176 | tf_op jit(solution)/shard_map/while/body/eval_jaxpr/ppermute | solution.py:13
  413.4 9.6 %collective-permute-done.4 = f32[2,8,4096]{2,1,0:T(8,128)S(1)} collective-permute-done((f32[2,8,4096]{2,1,0:T(8,128)S(1)}, f32[2,8,4096]{2,1,0:T(8,128)S(1)}, u32[]{:S(2)}, u32[]{:S(2)}) %collective-permute-start.4) | collective-permute-done | bytes 262176 | tf_op jit(solution)/shard_map/while/body/eval_jaxpr/ppermute | solution.py:13
  423.1 10.4 %collective-permute-start.5 = (f32[2,8,4096]{2,1,0:T(8,128)S(1)}, f32[2,8,4096]{2,1,0:T(8,128)S(1)}, u32[]{:S(2)}, u32[]{:S(2)}) collective-permute-start(f32[2,8,4096]{2,1,0:T(8,128)S(1)} %broadcast_select_fusion.18), channel_id=1, source_target_pairs={{0,32},{1,33},{2,34},{3,35},{4,36},{5,37},{6,38},{7,39},{8,40},{9,... | collective-permute-start | bytes 786440 | tf_op jit(solution)/shard_map/while/body/eval_jaxpr/ppermute | solution.py:13
  446.6 10.0 %collective-permute-done = f32[2,8,4096]{2,1,0:T(8,128)S(1)} collective-permute-done((f32[2,8,4096]{2,1,0:T(8,128)S(1)}, f32[2,8,4096]{2,1,0:T(8,128)S(1)}, u32[]{:S(2)}, u32[]{:S(2)}) %collective-permute-start) | collective-permute-done | bytes 262176 | tf_op jit(solution)/shard_map/while/body/eval_jaxpr/ppermute | solution.py:13
  456.8 10.3 %collective-permute-done.1 = f32[2,8,4096]{2,1,0:T(8,128)S(1)} collective-permute-done((f32[2,8,4096]{2,1,0:T(8,128)S(1)}, f32[2,8,4096]{2,1,0:T(8,128)S(1)}, u32[]{:S(2)}, u32[]{:S(2)}) %collective-permute-start.1) | collective-permute-done | bytes 262176 | tf_op jit(solution)/shard_map/while/body/eval_jaxpr/ppermute | solution.py:13
  475.4 9.8 %collective-permute-done.3 = f32[2,8,4096]{2,1,0:T(8,128)S(1)} collective-permute-done((f32[2,8,4096]{2,1,0:T(8,128)S(1)}, f32[2,8,4096]{2,1,0:T(8,128)S(1)}, u32[]{:S(2)}, u32[]{:S(2)}) %collective-permute-start.3) | collective-permute-done | bytes 262176 | tf_op jit(solution)/shard_map/while/body/eval_jaxpr/ppermute | solution.py:13
  485.4 9.6 %collective-permute-done.4 = f32[2,8,4096]{2,1,0:T(8,128)S(1)} collective-permute-done((f32[2,8,4096]{2,1,0:T(8,128)S(1)}, f32[2,8,4096]{2,1,0:T(8,128)S(1)}, u32[]{:S(2)}, u32[]{:S(2)}) %collective-permute-start.4) | collective-permute-done | bytes 262176 | tf_op jit(solution)/shard_map/while/body/eval_jaxpr/ppermute | solution.py:13
  495.0 10.4 %collective-permute-start.5 = (f32[2,8,4096]{2,1,0:T(8,128)S(1)}, f32[2,8,4096]{2,1,0:T(8,128)S(1)}, u32[]{:S(2)}, u32[]{:S(2)}) collective-permute-start(f32[2,8,4096]{2,1,0:T(8,128)S(1)} %broadcast_select_fusion.18), channel_id=1, source_target_pairs={{0,32},{1,33},{2,34},{3,35},{4,36},{5,37},{6,38},{7,39},{8,40},{9,... | collective-permute-start | bytes 786440 | tf_op jit(solution)/shard_map/while/body/eval_jaxpr/ppermute | solution.py:13
  518.6 10.0 %collective-permute-done = f32[2,8,4096]{2,1,0:T(8,128)S(1)} collective-permute-done((f32[2,8,4096]{2,1,0:T(8,128)S(1)}, f32[2,8,4096]{2,1,0:T(8,128)S(1)}, u32[]{:S(2)}, u32[]{:S(2)}) %collective-permute-start) | collective-permute-done | bytes 262176 | tf_op jit(solution)/shard_map/while/body/eval_jaxpr/ppermute | solution.py:13
  528.7 10.3 %collective-permute-done.1 = f32[2,8,4096]{2,1,0:T(8,128)S(1)} collective-permute-done((f32[2,8,4096]{2,1,0:T(8,128)S(1)}, f32[2,8,4096]{2,1,0:T(8,128)S(1)}, u32[]{:S(2)}, u32[]{:S(2)}) %collective-permute-start.1) | collective-permute-done | bytes 262176 | tf_op jit(solution)/shard_map/while/body/eval_jaxpr/ppermute | solution.py:13
  547.3 9.8 %collective-permute-done.3 = f32[2,8,4096]{2,1,0:T(8,128)S(1)} collective-permute-done((f32[2,8,4096]{2,1,0:T(8,128)S(1)}, f32[2,8,4096]{2,1,0:T(8,128)S(1)}, u32[]{:S(2)}, u32[]{:S(2)}) %collective-permute-start.3) | collective-permute-done | bytes 262176 | tf_op jit(solution)/shard_map/while/body/eval_jaxpr/ppermute | solution.py:13
  557.3 9.6 %collective-permute-done.4 = f32[2,8,4096]{2,1,0:T(8,128)S(1)} collective-permute-done((f32[2,8,4096]{2,1,0:T(8,128)S(1)}, f32[2,8,4096]{2,1,0:T(8,128)S(1)}, u32[]{:S(2)}, u32[]{:S(2)}) %collective-permute-start.4) | collective-permute-done | bytes 262176 | tf_op jit(solution)/shard_map/while/body/eval_jaxpr/ppermute | solution.py:13
  566.9 10.4 %collective-permute-start.5 = (f32[2,8,4096]{2,1,0:T(8,128)S(1)}, f32[2,8,4096]{2,1,0:T(8,128)S(1)}, u32[]{:S(2)}, u32[]{:S(2)}) collective-permute-start(f32[2,8,4096]{2,1,0:T(8,128)S(1)} %broadcast_select_fusion.18), channel_id=1, source_target_pairs={{0,32},{1,33},{2,34},{3,35},{4,36},{5,37},{6,38},{7,39},{8,40},{9,... | collective-permute-start | bytes 786440 | tf_op jit(solution)/shard_map/while/body/eval_jaxpr/ppermute | solution.py:13
  590.5 10.0 %collective-permute-done = f32[2,8,4096]{2,1,0:T(8,128)S(1)} collective-permute-done((f32[2,8,4096]{2,1,0:T(8,128)S(1)}, f32[2,8,4096]{2,1,0:T(8,128)S(1)}, u32[]{:S(2)}, u32[]{:S(2)}) %collective-permute-start) | collective-permute-done | bytes 262176 | tf_op jit(solution)/shard_map/while/body/eval_jaxpr/ppermute | solution.py:13
  600.7 10.3 %collective-permute-done.1 = f32[2,8,4096]{2,1,0:T(8,128)S(1)} collective-permute-done((f32[2,8,4096]{2,1,0:T(8,128)S(1)}, f32[2,8,4096]{2,1,0:T(8,128)S(1)}, u32[]{:S(2)}, u32[]{:S(2)}) %collective-permute-start.1) | collective-permute-done | bytes 262176 | tf_op jit(solution)/shard_map/while/body/eval_jaxpr/ppermute | solution.py:13
  619.2 9.8 %collective-permute-done.3 = f32[2,8,4096]{2,1,0:T(8,128)S(1)} collective-permute-done((f32[2,8,4096]{2,1,0:T(8,128)S(1)}, f32[2,8,4096]{2,1,0:T(8,128)S(1)}, u32[]{:S(2)}, u32[]{:S(2)}) %collective-permute-start.3) | collective-permute-done | bytes 262176 | tf_op jit(solution)/shard_map/while/body/eval_jaxpr/ppermute | solution.py:13
  629.2 9.6 %collective-permute-done.4 = f32[2,8,4096]{2,1,0:T(8,128)S(1)} collective-permute-done((f32[2,8,4096]{2,1,0:T(8,128)S(1)}, f32[2,8,4096]{2,1,0:T(8,128)S(1)}, u32[]{:S(2)}, u32[]{:S(2)}) %collective-permute-start.4) | collective-permute-done | bytes 262176 | tf_op jit(solution)/shard_map/while/body/eval_jaxpr/ppermute | solution.py:13
  638.9 10.4 %collective-permute-start.5 = (f32[2,8,4096]{2,1,0:T(8,128)S(1)}, f32[2,8,4096]{2,1,0:T(8,128)S(1)}, u32[]{:S(2)}, u32[]{:S(2)}) collective-permute-start(f32[2,8,4096]{2,1,0:T(8,128)S(1)} %broadcast_select_fusion.18), channel_id=1, source_target_pairs={{0,32},{1,33},{2,34},{3,35},{4,36},{5,37},{6,38},{7,39},{8,40},{9,... | collective-permute-start | bytes 786440 | tf_op jit(solution)/shard_map/while/body/eval_jaxpr/ppermute | solution.py:13
  662.4 10.0 %collective-permute-done = f32[2,8,4096]{2,1,0:T(8,128)S(1)} collective-permute-done((f32[2,8,4096]{2,1,0:T(8,128)S(1)}, f32[2,8,4096]{2,1,0:T(8,128)S(1)}, u32[]{:S(2)}, u32[]{:S(2)}) %collective-permute-start) | collective-permute-done | bytes 262176 | tf_op jit(solution)/shard_map/while/body/eval_jaxpr/ppermute | solution.py:13
  672.6 10.3 %collective-permute-done.1 = f32[2,8,4096]{2,1,0:T(8,128)S(1)} collective-permute-done((f32[2,8,4096]{2,1,0:T(8,128)S(1)}, f32[2,8,4096]{2,1,0:T(8,128)S(1)}, u32[]{:S(2)}, u32[]{:S(2)}) %collective-permute-start.1) | collective-permute-done | bytes 262176 | tf_op jit(solution)/shard_map/while/body/eval_jaxpr/ppermute | solution.py:13
  691.1 9.8 %collective-permute-done.3 = f32[2,8,4096]{2,1,0:T(8,128)S(1)} collective-permute-done((f32[2,8,4096]{2,1,0:T(8,128)S(1)}, f32[2,8,4096]{2,1,0:T(8,128)S(1)}, u32[]{:S(2)}, u32[]{:S(2)}) %collective-permute-start.3) | collective-permute-done | bytes 262176 | tf_op jit(solution)/shard_map/while/body/eval_jaxpr/ppermute | solution.py:13
  701.1 9.6 %collective-permute-done.4 = f32[2,8,4096]{2,1,0:T(8,128)S(1)} collective-permute-done((f32[2,8,4096]{2,1,0:T(8,128)S(1)}, f32[2,8,4096]{2,1,0:T(8,128)S(1)}, u32[]{:S(2)}, u32[]{:S(2)}) %collective-permute-start.4) | collective-permute-done | bytes 262176 | tf_op jit(solution)/shard_map/while/body/eval_jaxpr/ppermute | solution.py:13
  710.8 10.4 %collective-permute-start.5 = (f32[2,8,4096]{2,1,0:T(8,128)S(1)}, f32[2,8,4096]{2,1,0:T(8,128)S(1)}, u32[]{:S(2)}, u32[]{:S(2)}) collective-permute-start(f32[2,8,4096]{2,1,0:T(8,128)S(1)} %broadcast_select_fusion.18), channel_id=1, source_target_pairs={{0,32},{1,33},{2,34},{3,35},{4,36},{5,37},{6,38},{7,39},{8,40},{9,... | collective-permute-start | bytes 786440 | tf_op jit(solution)/shard_map/while/body/eval_jaxpr/ppermute | solution.py:13
  (218 shorter events, 256.7 us)
Async XLA Ops:
  15.0 15.4 %collective-permute-start = (f32[2,8,4096]{2,1,0:T(8,128)S(1)}, f32[2,8,4096]{2,1,0:T(8,128)S(1)}, u32[]{:S(2)}, u32[]{:S(2)}) collective-permute-start(f32[2,8,4096]{2,1,0:T(8,128)S(1)} %bitcast_add_fusion.2), channel_id=1, source_target_pairs={{0,1},{1,2},{2,3},{3,4},{4,5},{5,6},{6,7},{7,8},{8,9},{9,10},{10,1... | collective-permute-start | bytes 786440 | tf_op jit(solution)/shard_map/while/body/eval_jaxpr/ppermute | solution.py:13
  30.5 12.9 %collective-permute-start.1 = (f32[2,8,4096]{2,1,0:T(8,128)S(1)}, f32[2,8,4096]{2,1,0:T(8,128)S(1)}, u32[]{:S(2)}, u32[]{:S(2)}) collective-permute-start(f32[2,8,4096]{2,1,0:T(8,128)S(1)} %broadcast_select_fusion.14), channel_id=1, source_target_pairs={{0,2},{1,3},{2,4},{3,5},{4,6},{5,7},{6,8},{7,9},{8,10},{9,11},{10,... | collective-permute-start | bytes 786440 | tf_op jit(solution)/shard_map/while/body/eval_jaxpr/ppermute | solution.py:13
  75.7 10.0 %collective-permute-start.6 = (f32[2,8,4096]{2,1,0:T(8,128)S(1)}, f32[2,8,4096]{2,1,0:T(8,128)S(1)}, u32[]{:S(2)}, u32[]{:S(2)}) collective-permute-start(f32[2,8,4096]{2,1,0:T(8,128)S(1)} %broadcast_select_fusion.19), channel_id=1, source_target_pairs={{0,64},{1,65},{2,66},{3,67},{4,68},{5,69},{6,70},{7,71},{8,72},{9,... | collective-permute-start | bytes 786440 | tf_op jit(solution)/shard_map/while/body/eval_jaxpr/ppermute | solution.py:13
  86.9 10.1 %collective-permute-start = (f32[2,8,4096]{2,1,0:T(8,128)S(1)}, f32[2,8,4096]{2,1,0:T(8,128)S(1)}, u32[]{:S(2)}, u32[]{:S(2)}) collective-permute-start(f32[2,8,4096]{2,1,0:T(8,128)S(1)} %bitcast_add_fusion.2), channel_id=1, source_target_pairs={{0,1},{1,2},{2,3},{3,4},{4,5},{5,6},{6,7},{7,8},{8,9},{9,10},{10,1... | collective-permute-start | bytes 786440 | tf_op jit(solution)/shard_map/while/body/eval_jaxpr/ppermute | solution.py:13
  97.1 10.4 %collective-permute-start.1 = (f32[2,8,4096]{2,1,0:T(8,128)S(1)}, f32[2,8,4096]{2,1,0:T(8,128)S(1)}, u32[]{:S(2)}, u32[]{:S(2)}) collective-permute-start(f32[2,8,4096]{2,1,0:T(8,128)S(1)} %broadcast_select_fusion.14), channel_id=1, source_target_pairs={{0,2},{1,3},{2,4},{3,5},{4,6},{5,7},{6,8},{7,9},{8,10},{9,11},{10,... | collective-permute-start | bytes 786440 | tf_op jit(solution)/shard_map/while/body/eval_jaxpr/ppermute | solution.py:13
  115.6 9.9 %collective-permute-start.3 = (f32[2,8,4096]{2,1,0:T(8,128)S(1)}, f32[2,8,4096]{2,1,0:T(8,128)S(1)}, u32[]{:S(2)}, u32[]{:S(2)}) collective-permute-start(f32[2,8,4096]{2,1,0:T(8,128)S(1)} %broadcast_select_fusion.16), channel_id=1, source_target_pairs={{0,8},{1,9},{2,10},{3,11},{4,12},{5,13},{6,14},{7,15},{8,16},{9,17... | collective-permute-start | bytes 786440 | tf_op jit(solution)/shard_map/while/body/eval_jaxpr/ppermute | solution.py:13
  125.6 9.7 %collective-permute-start.4 = (f32[2,8,4096]{2,1,0:T(8,128)S(1)}, f32[2,8,4096]{2,1,0:T(8,128)S(1)}, u32[]{:S(2)}, u32[]{:S(2)}) collective-permute-start(f32[2,8,4096]{2,1,0:T(8,128)S(1)} %broadcast_select_fusion.17), channel_id=1, source_target_pairs={{0,16},{1,17},{2,18},{3,19},{4,20},{5,21},{6,22},{7,23},{8,24},{9,... | collective-permute-start | bytes 786440 | tf_op jit(solution)/shard_map/while/body/eval_jaxpr/ppermute | solution.py:13
  135.4 13.8 %collective-permute-start.5 = (f32[2,8,4096]{2,1,0:T(8,128)S(1)}, f32[2,8,4096]{2,1,0:T(8,128)S(1)}, u32[]{:S(2)}, u32[]{:S(2)}) collective-permute-start(f32[2,8,4096]{2,1,0:T(8,128)S(1)} %broadcast_select_fusion.18), channel_id=1, source_target_pairs={{0,32},{1,33},{2,34},{3,35},{4,36},{5,37},{6,38},{7,39},{8,40},{9,... | collective-permute-start | bytes 786440 | tf_op jit(solution)/shard_map/while/body/eval_jaxpr/ppermute | solution.py:13
  158.8 10.1 %collective-permute-start = (f32[2,8,4096]{2,1,0:T(8,128)S(1)}, f32[2,8,4096]{2,1,0:T(8,128)S(1)}, u32[]{:S(2)}, u32[]{:S(2)}) collective-permute-start(f32[2,8,4096]{2,1,0:T(8,128)S(1)} %bitcast_add_fusion.2), channel_id=1, source_target_pairs={{0,1},{1,2},{2,3},{3,4},{4,5},{5,6},{6,7},{7,8},{8,9},{9,10},{10,1... | collective-permute-start | bytes 786440 | tf_op jit(solution)/shard_map/while/body/eval_jaxpr/ppermute | solution.py:13
  169.0 10.4 %collective-permute-start.1 = (f32[2,8,4096]{2,1,0:T(8,128)S(1)}, f32[2,8,4096]{2,1,0:T(8,128)S(1)}, u32[]{:S(2)}, u32[]{:S(2)}) collective-permute-start(f32[2,8,4096]{2,1,0:T(8,128)S(1)} %broadcast_select_fusion.14), channel_id=1, source_target_pairs={{0,2},{1,3},{2,4},{3,5},{4,6},{5,7},{6,8},{7,9},{8,10},{9,11},{10,... | collective-permute-start | bytes 786440 | tf_op jit(solution)/shard_map/while/body/eval_jaxpr/ppermute | solution.py:13
  187.6 9.9 %collective-permute-start.3 = (f32[2,8,4096]{2,1,0:T(8,128)S(1)}, f32[2,8,4096]{2,1,0:T(8,128)S(1)}, u32[]{:S(2)}, u32[]{:S(2)}) collective-permute-start(f32[2,8,4096]{2,1,0:T(8,128)S(1)} %broadcast_select_fusion.16), channel_id=1, source_target_pairs={{0,8},{1,9},{2,10},{3,11},{4,12},{5,13},{6,14},{7,15},{8,16},{9,17... | collective-permute-start | bytes 786440 | tf_op jit(solution)/shard_map/while/body/eval_jaxpr/ppermute | solution.py:13
  197.5 9.7 %collective-permute-start.4 = (f32[2,8,4096]{2,1,0:T(8,128)S(1)}, f32[2,8,4096]{2,1,0:T(8,128)S(1)}, u32[]{:S(2)}, u32[]{:S(2)}) collective-permute-start(f32[2,8,4096]{2,1,0:T(8,128)S(1)} %broadcast_select_fusion.17), channel_id=1, source_target_pairs={{0,16},{1,17},{2,18},{3,19},{4,20},{5,21},{6,22},{7,23},{8,24},{9,... | collective-permute-start | bytes 786440 | tf_op jit(solution)/shard_map/while/body/eval_jaxpr/ppermute | solution.py:13
  207.3 13.8 %collective-permute-start.5 = (f32[2,8,4096]{2,1,0:T(8,128)S(1)}, f32[2,8,4096]{2,1,0:T(8,128)S(1)}, u32[]{:S(2)}, u32[]{:S(2)}) collective-permute-start(f32[2,8,4096]{2,1,0:T(8,128)S(1)} %broadcast_select_fusion.18), channel_id=1, source_target_pairs={{0,32},{1,33},{2,34},{3,35},{4,36},{5,37},{6,38},{7,39},{8,40},{9,... | collective-permute-start | bytes 786440 | tf_op jit(solution)/shard_map/while/body/eval_jaxpr/ppermute | solution.py:13
  230.7 10.1 %collective-permute-start = (f32[2,8,4096]{2,1,0:T(8,128)S(1)}, f32[2,8,4096]{2,1,0:T(8,128)S(1)}, u32[]{:S(2)}, u32[]{:S(2)}) collective-permute-start(f32[2,8,4096]{2,1,0:T(8,128)S(1)} %bitcast_add_fusion.2), channel_id=1, source_target_pairs={{0,1},{1,2},{2,3},{3,4},{4,5},{5,6},{6,7},{7,8},{8,9},{9,10},{10,1... | collective-permute-start | bytes 786440 | tf_op jit(solution)/shard_map/while/body/eval_jaxpr/ppermute | solution.py:13
  240.9 10.4 %collective-permute-start.1 = (f32[2,8,4096]{2,1,0:T(8,128)S(1)}, f32[2,8,4096]{2,1,0:T(8,128)S(1)}, u32[]{:S(2)}, u32[]{:S(2)}) collective-permute-start(f32[2,8,4096]{2,1,0:T(8,128)S(1)} %broadcast_select_fusion.14), channel_id=1, source_target_pairs={{0,2},{1,3},{2,4},{3,5},{4,6},{5,7},{6,8},{7,9},{8,10},{9,11},{10,... | collective-permute-start | bytes 786440 | tf_op jit(solution)/shard_map/while/body/eval_jaxpr/ppermute | solution.py:13
  259.5 9.9 %collective-permute-start.3 = (f32[2,8,4096]{2,1,0:T(8,128)S(1)}, f32[2,8,4096]{2,1,0:T(8,128)S(1)}, u32[]{:S(2)}, u32[]{:S(2)}) collective-permute-start(f32[2,8,4096]{2,1,0:T(8,128)S(1)} %broadcast_select_fusion.16), channel_id=1, source_target_pairs={{0,8},{1,9},{2,10},{3,11},{4,12},{5,13},{6,14},{7,15},{8,16},{9,17... | collective-permute-start | bytes 786440 | tf_op jit(solution)/shard_map/while/body/eval_jaxpr/ppermute | solution.py:13
  269.5 9.7 %collective-permute-start.4 = (f32[2,8,4096]{2,1,0:T(8,128)S(1)}, f32[2,8,4096]{2,1,0:T(8,128)S(1)}, u32[]{:S(2)}, u32[]{:S(2)}) collective-permute-start(f32[2,8,4096]{2,1,0:T(8,128)S(1)} %broadcast_select_fusion.17), channel_id=1, source_target_pairs={{0,16},{1,17},{2,18},{3,19},{4,20},{5,21},{6,22},{7,23},{8,24},{9,... | collective-permute-start | bytes 786440 | tf_op jit(solution)/shard_map/while/body/eval_jaxpr/ppermute | solution.py:13
  279.2 13.8 %collective-permute-start.5 = (f32[2,8,4096]{2,1,0:T(8,128)S(1)}, f32[2,8,4096]{2,1,0:T(8,128)S(1)}, u32[]{:S(2)}, u32[]{:S(2)}) collective-permute-start(f32[2,8,4096]{2,1,0:T(8,128)S(1)} %broadcast_select_fusion.18), channel_id=1, source_target_pairs={{0,32},{1,33},{2,34},{3,35},{4,36},{5,37},{6,38},{7,39},{8,40},{9,... | collective-permute-start | bytes 786440 | tf_op jit(solution)/shard_map/while/body/eval_jaxpr/ppermute | solution.py:13
  302.7 10.1 %collective-permute-start = (f32[2,8,4096]{2,1,0:T(8,128)S(1)}, f32[2,8,4096]{2,1,0:T(8,128)S(1)}, u32[]{:S(2)}, u32[]{:S(2)}) collective-permute-start(f32[2,8,4096]{2,1,0:T(8,128)S(1)} %bitcast_add_fusion.2), channel_id=1, source_target_pairs={{0,1},{1,2},{2,3},{3,4},{4,5},{5,6},{6,7},{7,8},{8,9},{9,10},{10,1... | collective-permute-start | bytes 786440 | tf_op jit(solution)/shard_map/while/body/eval_jaxpr/ppermute | solution.py:13
  312.9 10.4 %collective-permute-start.1 = (f32[2,8,4096]{2,1,0:T(8,128)S(1)}, f32[2,8,4096]{2,1,0:T(8,128)S(1)}, u32[]{:S(2)}, u32[]{:S(2)}) collective-permute-start(f32[2,8,4096]{2,1,0:T(8,128)S(1)} %broadcast_select_fusion.14), channel_id=1, source_target_pairs={{0,2},{1,3},{2,4},{3,5},{4,6},{5,7},{6,8},{7,9},{8,10},{9,11},{10,... | collective-permute-start | bytes 786440 | tf_op jit(solution)/shard_map/while/body/eval_jaxpr/ppermute | solution.py:13
  331.4 9.9 %collective-permute-start.3 = (f32[2,8,4096]{2,1,0:T(8,128)S(1)}, f32[2,8,4096]{2,1,0:T(8,128)S(1)}, u32[]{:S(2)}, u32[]{:S(2)}) collective-permute-start(f32[2,8,4096]{2,1,0:T(8,128)S(1)} %broadcast_select_fusion.16), channel_id=1, source_target_pairs={{0,8},{1,9},{2,10},{3,11},{4,12},{5,13},{6,14},{7,15},{8,16},{9,17... | collective-permute-start | bytes 786440 | tf_op jit(solution)/shard_map/while/body/eval_jaxpr/ppermute | solution.py:13
  341.4 9.7 %collective-permute-start.4 = (f32[2,8,4096]{2,1,0:T(8,128)S(1)}, f32[2,8,4096]{2,1,0:T(8,128)S(1)}, u32[]{:S(2)}, u32[]{:S(2)}) collective-permute-start(f32[2,8,4096]{2,1,0:T(8,128)S(1)} %broadcast_select_fusion.17), channel_id=1, source_target_pairs={{0,16},{1,17},{2,18},{3,19},{4,20},{5,21},{6,22},{7,23},{8,24},{9,... | collective-permute-start | bytes 786440 | tf_op jit(solution)/shard_map/while/body/eval_jaxpr/ppermute | solution.py:13
  351.2 13.8 %collective-permute-start.5 = (f32[2,8,4096]{2,1,0:T(8,128)S(1)}, f32[2,8,4096]{2,1,0:T(8,128)S(1)}, u32[]{:S(2)}, u32[]{:S(2)}) collective-permute-start(f32[2,8,4096]{2,1,0:T(8,128)S(1)} %broadcast_select_fusion.18), channel_id=1, source_target_pairs={{0,32},{1,33},{2,34},{3,35},{4,36},{5,37},{6,38},{7,39},{8,40},{9,... | collective-permute-start | bytes 786440 | tf_op jit(solution)/shard_map/while/body/eval_jaxpr/ppermute | solution.py:13
  374.6 10.1 %collective-permute-start = (f32[2,8,4096]{2,1,0:T(8,128)S(1)}, f32[2,8,4096]{2,1,0:T(8,128)S(1)}, u32[]{:S(2)}, u32[]{:S(2)}) collective-permute-start(f32[2,8,4096]{2,1,0:T(8,128)S(1)} %bitcast_add_fusion.2), channel_id=1, source_target_pairs={{0,1},{1,2},{2,3},{3,4},{4,5},{5,6},{6,7},{7,8},{8,9},{9,10},{10,1... | collective-permute-start | bytes 786440 | tf_op jit(solution)/shard_map/while/body/eval_jaxpr/ppermute | solution.py:13
  384.8 10.4 %collective-permute-start.1 = (f32[2,8,4096]{2,1,0:T(8,128)S(1)}, f32[2,8,4096]{2,1,0:T(8,128)S(1)}, u32[]{:S(2)}, u32[]{:S(2)}) collective-permute-start(f32[2,8,4096]{2,1,0:T(8,128)S(1)} %broadcast_select_fusion.14), channel_id=1, source_target_pairs={{0,2},{1,3},{2,4},{3,5},{4,6},{5,7},{6,8},{7,9},{8,10},{9,11},{10,... | collective-permute-start | bytes 786440 | tf_op jit(solution)/shard_map/while/body/eval_jaxpr/ppermute | solution.py:13
  403.3 9.9 %collective-permute-start.3 = (f32[2,8,4096]{2,1,0:T(8,128)S(1)}, f32[2,8,4096]{2,1,0:T(8,128)S(1)}, u32[]{:S(2)}, u32[]{:S(2)}) collective-permute-start(f32[2,8,4096]{2,1,0:T(8,128)S(1)} %broadcast_select_fusion.16), channel_id=1, source_target_pairs={{0,8},{1,9},{2,10},{3,11},{4,12},{5,13},{6,14},{7,15},{8,16},{9,17... | collective-permute-start | bytes 786440 | tf_op jit(solution)/shard_map/while/body/eval_jaxpr/ppermute | solution.py:13
  413.3 9.7 %collective-permute-start.4 = (f32[2,8,4096]{2,1,0:T(8,128)S(1)}, f32[2,8,4096]{2,1,0:T(8,128)S(1)}, u32[]{:S(2)}, u32[]{:S(2)}) collective-permute-start(f32[2,8,4096]{2,1,0:T(8,128)S(1)} %broadcast_select_fusion.17), channel_id=1, source_target_pairs={{0,16},{1,17},{2,18},{3,19},{4,20},{5,21},{6,22},{7,23},{8,24},{9,... | collective-permute-start | bytes 786440 | tf_op jit(solution)/shard_map/while/body/eval_jaxpr/ppermute | solution.py:13
  423.1 13.8 %collective-permute-start.5 = (f32[2,8,4096]{2,1,0:T(8,128)S(1)}, f32[2,8,4096]{2,1,0:T(8,128)S(1)}, u32[]{:S(2)}, u32[]{:S(2)}) collective-permute-start(f32[2,8,4096]{2,1,0:T(8,128)S(1)} %broadcast_select_fusion.18), channel_id=1, source_target_pairs={{0,32},{1,33},{2,34},{3,35},{4,36},{5,37},{6,38},{7,39},{8,40},{9,... | collective-permute-start | bytes 786440 | tf_op jit(solution)/shard_map/while/body/eval_jaxpr/ppermute | solution.py:13
  446.5 10.1 %collective-permute-start = (f32[2,8,4096]{2,1,0:T(8,128)S(1)}, f32[2,8,4096]{2,1,0:T(8,128)S(1)}, u32[]{:S(2)}, u32[]{:S(2)}) collective-permute-start(f32[2,8,4096]{2,1,0:T(8,128)S(1)} %bitcast_add_fusion.2), channel_id=1, source_target_pairs={{0,1},{1,2},{2,3},{3,4},{4,5},{5,6},{6,7},{7,8},{8,9},{9,10},{10,1... | collective-permute-start | bytes 786440 | tf_op jit(solution)/shard_map/while/body/eval_jaxpr/ppermute | solution.py:13
  456.7 10.4 %collective-permute-start.1 = (f32[2,8,4096]{2,1,0:T(8,128)S(1)}, f32[2,8,4096]{2,1,0:T(8,128)S(1)}, u32[]{:S(2)}, u32[]{:S(2)}) collective-permute-start(f32[2,8,4096]{2,1,0:T(8,128)S(1)} %broadcast_select_fusion.14), channel_id=1, source_target_pairs={{0,2},{1,3},{2,4},{3,5},{4,6},{5,7},{6,8},{7,9},{8,10},{9,11},{10,... | collective-permute-start | bytes 786440 | tf_op jit(solution)/shard_map/while/body/eval_jaxpr/ppermute | solution.py:13
  475.3 9.9 %collective-permute-start.3 = (f32[2,8,4096]{2,1,0:T(8,128)S(1)}, f32[2,8,4096]{2,1,0:T(8,128)S(1)}, u32[]{:S(2)}, u32[]{:S(2)}) collective-permute-start(f32[2,8,4096]{2,1,0:T(8,128)S(1)} %broadcast_select_fusion.16), channel_id=1, source_target_pairs={{0,8},{1,9},{2,10},{3,11},{4,12},{5,13},{6,14},{7,15},{8,16},{9,17... | collective-permute-start | bytes 786440 | tf_op jit(solution)/shard_map/while/body/eval_jaxpr/ppermute | solution.py:13
  485.3 9.7 %collective-permute-start.4 = (f32[2,8,4096]{2,1,0:T(8,128)S(1)}, f32[2,8,4096]{2,1,0:T(8,128)S(1)}, u32[]{:S(2)}, u32[]{:S(2)}) collective-permute-start(f32[2,8,4096]{2,1,0:T(8,128)S(1)} %broadcast_select_fusion.17), channel_id=1, source_target_pairs={{0,16},{1,17},{2,18},{3,19},{4,20},{5,21},{6,22},{7,23},{8,24},{9,... | collective-permute-start | bytes 786440 | tf_op jit(solution)/shard_map/while/body/eval_jaxpr/ppermute | solution.py:13
  495.0 13.8 %collective-permute-start.5 = (f32[2,8,4096]{2,1,0:T(8,128)S(1)}, f32[2,8,4096]{2,1,0:T(8,128)S(1)}, u32[]{:S(2)}, u32[]{:S(2)}) collective-permute-start(f32[2,8,4096]{2,1,0:T(8,128)S(1)} %broadcast_select_fusion.18), channel_id=1, source_target_pairs={{0,32},{1,33},{2,34},{3,35},{4,36},{5,37},{6,38},{7,39},{8,40},{9,... | collective-permute-start | bytes 786440 | tf_op jit(solution)/shard_map/while/body/eval_jaxpr/ppermute | solution.py:13
  518.4 10.1 %collective-permute-start = (f32[2,8,4096]{2,1,0:T(8,128)S(1)}, f32[2,8,4096]{2,1,0:T(8,128)S(1)}, u32[]{:S(2)}, u32[]{:S(2)}) collective-permute-start(f32[2,8,4096]{2,1,0:T(8,128)S(1)} %bitcast_add_fusion.2), channel_id=1, source_target_pairs={{0,1},{1,2},{2,3},{3,4},{4,5},{5,6},{6,7},{7,8},{8,9},{9,10},{10,1... | collective-permute-start | bytes 786440 | tf_op jit(solution)/shard_map/while/body/eval_jaxpr/ppermute | solution.py:13
  528.6 10.4 %collective-permute-start.1 = (f32[2,8,4096]{2,1,0:T(8,128)S(1)}, f32[2,8,4096]{2,1,0:T(8,128)S(1)}, u32[]{:S(2)}, u32[]{:S(2)}) collective-permute-start(f32[2,8,4096]{2,1,0:T(8,128)S(1)} %broadcast_select_fusion.14), channel_id=1, source_target_pairs={{0,2},{1,3},{2,4},{3,5},{4,6},{5,7},{6,8},{7,9},{8,10},{9,11},{10,... | collective-permute-start | bytes 786440 | tf_op jit(solution)/shard_map/while/body/eval_jaxpr/ppermute | solution.py:13
  547.2 9.9 %collective-permute-start.3 = (f32[2,8,4096]{2,1,0:T(8,128)S(1)}, f32[2,8,4096]{2,1,0:T(8,128)S(1)}, u32[]{:S(2)}, u32[]{:S(2)}) collective-permute-start(f32[2,8,4096]{2,1,0:T(8,128)S(1)} %broadcast_select_fusion.16), channel_id=1, source_target_pairs={{0,8},{1,9},{2,10},{3,11},{4,12},{5,13},{6,14},{7,15},{8,16},{9,17... | collective-permute-start | bytes 786440 | tf_op jit(solution)/shard_map/while/body/eval_jaxpr/ppermute | solution.py:13
  557.2 9.7 %collective-permute-start.4 = (f32[2,8,4096]{2,1,0:T(8,128)S(1)}, f32[2,8,4096]{2,1,0:T(8,128)S(1)}, u32[]{:S(2)}, u32[]{:S(2)}) collective-permute-start(f32[2,8,4096]{2,1,0:T(8,128)S(1)} %broadcast_select_fusion.17), channel_id=1, source_target_pairs={{0,16},{1,17},{2,18},{3,19},{4,20},{5,21},{6,22},{7,23},{8,24},{9,... | collective-permute-start | bytes 786440 | tf_op jit(solution)/shard_map/while/body/eval_jaxpr/ppermute | solution.py:13
  566.9 13.8 %collective-permute-start.5 = (f32[2,8,4096]{2,1,0:T(8,128)S(1)}, f32[2,8,4096]{2,1,0:T(8,128)S(1)}, u32[]{:S(2)}, u32[]{:S(2)}) collective-permute-start(f32[2,8,4096]{2,1,0:T(8,128)S(1)} %broadcast_select_fusion.18), channel_id=1, source_target_pairs={{0,32},{1,33},{2,34},{3,35},{4,36},{5,37},{6,38},{7,39},{8,40},{9,... | collective-permute-start | bytes 786440 | tf_op jit(solution)/shard_map/while/body/eval_jaxpr/ppermute | solution.py:13
  590.4 10.1 %collective-permute-start = (f32[2,8,4096]{2,1,0:T(8,128)S(1)}, f32[2,8,4096]{2,1,0:T(8,128)S(1)}, u32[]{:S(2)}, u32[]{:S(2)}) collective-permute-start(f32[2,8,4096]{2,1,0:T(8,128)S(1)} %bitcast_add_fusion.2), channel_id=1, source_target_pairs={{0,1},{1,2},{2,3},{3,4},{4,5},{5,6},{6,7},{7,8},{8,9},{9,10},{10,1... | collective-permute-start | bytes 786440 | tf_op jit(solution)/shard_map/while/body/eval_jaxpr/ppermute | solution.py:13
  600.6 10.4 %collective-permute-start.1 = (f32[2,8,4096]{2,1,0:T(8,128)S(1)}, f32[2,8,4096]{2,1,0:T(8,128)S(1)}, u32[]{:S(2)}, u32[]{:S(2)}) collective-permute-start(f32[2,8,4096]{2,1,0:T(8,128)S(1)} %broadcast_select_fusion.14), channel_id=1, source_target_pairs={{0,2},{1,3},{2,4},{3,5},{4,6},{5,7},{6,8},{7,9},{8,10},{9,11},{10,... | collective-permute-start | bytes 786440 | tf_op jit(solution)/shard_map/while/body/eval_jaxpr/ppermute | solution.py:13
  619.1 9.9 %collective-permute-start.3 = (f32[2,8,4096]{2,1,0:T(8,128)S(1)}, f32[2,8,4096]{2,1,0:T(8,128)S(1)}, u32[]{:S(2)}, u32[]{:S(2)}) collective-permute-start(f32[2,8,4096]{2,1,0:T(8,128)S(1)} %broadcast_select_fusion.16), channel_id=1, source_target_pairs={{0,8},{1,9},{2,10},{3,11},{4,12},{5,13},{6,14},{7,15},{8,16},{9,17... | collective-permute-start | bytes 786440 | tf_op jit(solution)/shard_map/while/body/eval_jaxpr/ppermute | solution.py:13
  629.1 9.7 %collective-permute-start.4 = (f32[2,8,4096]{2,1,0:T(8,128)S(1)}, f32[2,8,4096]{2,1,0:T(8,128)S(1)}, u32[]{:S(2)}, u32[]{:S(2)}) collective-permute-start(f32[2,8,4096]{2,1,0:T(8,128)S(1)} %broadcast_select_fusion.17), channel_id=1, source_target_pairs={{0,16},{1,17},{2,18},{3,19},{4,20},{5,21},{6,22},{7,23},{8,24},{9,... | collective-permute-start | bytes 786440 | tf_op jit(solution)/shard_map/while/body/eval_jaxpr/ppermute | solution.py:13
  638.9 13.8 %collective-permute-start.5 = (f32[2,8,4096]{2,1,0:T(8,128)S(1)}, f32[2,8,4096]{2,1,0:T(8,128)S(1)}, u32[]{:S(2)}, u32[]{:S(2)}) collective-permute-start(f32[2,8,4096]{2,1,0:T(8,128)S(1)} %broadcast_select_fusion.18), channel_id=1, source_target_pairs={{0,32},{1,33},{2,34},{3,35},{4,36},{5,37},{6,38},{7,39},{8,40},{9,... | collective-permute-start | bytes 786440 | tf_op jit(solution)/shard_map/while/body/eval_jaxpr/ppermute | solution.py:13
  662.3 10.1 %collective-permute-start = (f32[2,8,4096]{2,1,0:T(8,128)S(1)}, f32[2,8,4096]{2,1,0:T(8,128)S(1)}, u32[]{:S(2)}, u32[]{:S(2)}) collective-permute-start(f32[2,8,4096]{2,1,0:T(8,128)S(1)} %bitcast_add_fusion.2), channel_id=1, source_target_pairs={{0,1},{1,2},{2,3},{3,4},{4,5},{5,6},{6,7},{7,8},{8,9},{9,10},{10,1... | collective-permute-start | bytes 786440 | tf_op jit(solution)/shard_map/while/body/eval_jaxpr/ppermute | solution.py:13
  672.5 10.4 %collective-permute-start.1 = (f32[2,8,4096]{2,1,0:T(8,128)S(1)}, f32[2,8,4096]{2,1,0:T(8,128)S(1)}, u32[]{:S(2)}, u32[]{:S(2)}) collective-permute-start(f32[2,8,4096]{2,1,0:T(8,128)S(1)} %broadcast_select_fusion.14), channel_id=1, source_target_pairs={{0,2},{1,3},{2,4},{3,5},{4,6},{5,7},{6,8},{7,9},{8,10},{9,11},{10,... | collective-permute-start | bytes 786440 | tf_op jit(solution)/shard_map/while/body/eval_jaxpr/ppermute | solution.py:13
  691.1 9.9 %collective-permute-start.3 = (f32[2,8,4096]{2,1,0:T(8,128)S(1)}, f32[2,8,4096]{2,1,0:T(8,128)S(1)}, u32[]{:S(2)}, u32[]{:S(2)}) collective-permute-start(f32[2,8,4096]{2,1,0:T(8,128)S(1)} %broadcast_select_fusion.16), channel_id=1, source_target_pairs={{0,8},{1,9},{2,10},{3,11},{4,12},{5,13},{6,14},{7,15},{8,16},{9,17... | collective-permute-start | bytes 786440 | tf_op jit(solution)/shard_map/while/body/eval_jaxpr/ppermute | solution.py:13
  701.1 9.7 %collective-permute-start.4 = (f32[2,8,4096]{2,1,0:T(8,128)S(1)}, f32[2,8,4096]{2,1,0:T(8,128)S(1)}, u32[]{:S(2)}, u32[]{:S(2)}) collective-permute-start(f32[2,8,4096]{2,1,0:T(8,128)S(1)} %broadcast_select_fusion.17), channel_id=1, source_target_pairs={{0,16},{1,17},{2,18},{3,19},{4,20},{5,21},{6,22},{7,23},{8,24},{9,... | collective-permute-start | bytes 786440 | tf_op jit(solution)/shard_map/while/body/eval_jaxpr/ppermute | solution.py:13
  710.8 13.8 %collective-permute-start.5 = (f32[2,8,4096]{2,1,0:T(8,128)S(1)}, f32[2,8,4096]{2,1,0:T(8,128)S(1)}, u32[]{:S(2)}, u32[]{:S(2)}) collective-permute-start(f32[2,8,4096]{2,1,0:T(8,128)S(1)} %broadcast_select_fusion.18), channel_id=1, source_target_pairs={{0,32},{1,33},{2,34},{3,35},{4,36},{5,37},{6,38},{7,39},{8,40},{9,... | collective-permute-start | bytes 786440 | tf_op jit(solution)/shard_map/while/body/eval_jaxpr/ppermute | solution.py:13
  (25 other events, 200.2 us)
where the time goes:
time: 737 us; the launch traced here: 734 us
  waiting for transfers between devices  559 us (76%)
  starting transfers between devices  143 us (19%)
  other arithmetic  16.8 us (2%)
  local copies, waits for them, and re-layouts  12.6 us (2%)
    ppermute x70, waiting for transfers between devices, from_behind(): return lax.ppermute(value, axis, pairs)  559 us
    ppermute x70, starting transfers between devices, from_behind(): return lax.ppermute(value, axis, pairs)  143 us
  transfers between devices with their start and end apart: 70, of which 70 were waited for; matrix products, arithmetic and copies ran while one was open for 0% of the time, Pallas kernels for 0%

commit v1 on v0

v1 whole, which is shorter than its diff:
```python
import jax
import jax.numpy as jnp
from jax import lax
from jax.sharding import PartitionSpec as P

HELPERS = 10
REP_DEV = 2
AXES = ("rack", "node")


def on_device(stored, coefficients, helper_rack, helper_node, helper_block):
    node_count = lax.axis_size("node")
    device_count = lax.axis_size(AXES)
    planes, length = stored.shape[1:]
    my_device = lax.axis_index("rack") * node_count + lax.axis_index("node")
    offsets = (helper_rack[:REP_DEV] * node_count + helper_node[:REP_DEV]) % device_count
    owner = (my_device - offsets) % device_count
    position = jnp.arange(REP_DEV, dtype=jnp.int32)[:, None]
    repair_rows = owner * REP_DEV + position
    helper_slot = jnp.arange(HELPERS, dtype=jnp.int32)[None, :]
    local_rows = helper_block[repair_rows, helper_slot]
    coeffs_used = coefficients[repair_rows, helper_slot]
    blocks_used = stored[local_rows]
    contrib = jnp.einsum(
        "shpq,shql->shpl", coeffs_used, blocks_used, preferred_element_type=jnp.float32
    )
    terms = REP_DEV * HELPERS
    share = planes * length // device_count
    lanes = 128
    sent = contrib.reshape(terms, device_count, share).transpose(1, 0, 2)
    sent = sent.reshape(device_count, terms * share // lanes, lanes)
    held = lax.all_to_all(sent, AXES, 0, 0, tiled=True)
    held = held.reshape(device_count, terms, share // lanes, lanes)
    twice = jnp.concatenate([held, held], 0)
    sums = []
    for s in range(REP_DEV):
        total = None
        for h in range(HELPERS):
            part = lax.dynamic_slice(
                twice, (offsets[s, h], s * HELPERS + h, 0, 0), (device_count, 1, share // lanes, lanes)
            )
            total = part if total is None else total + part
        sums.append(total)
    back = jnp.concatenate(sums, 1).reshape(device_count, REP_DEV * share // lanes, lanes)
    rebuilt = lax.all_to_all(back, AXES, 0, 0, tiled=True)
    rebuilt = rebuilt.reshape(device_count, REP_DEV, share).transpose(1, 0, 2)
    return rebuilt.reshape(REP_DEV, planes, length)


def solution(mesh):
    placed = (P(AXES, None, None), P(), P(), P(), P())
    return jax.shard_map(
        on_device,
        mesh=mesh,
        in_specs=placed,
        out_specs=P(AXES, None, None),
        check_vma=False,
    )
```

time: 737 us -> 104 us (0.14)
  waiting for transfers between devices: 559 us -> 0.01 us
  starting transfers between devices: 143 us -> 11.9 us
  between operations: 0.05 us -> 37.9 us
  blocking collectives: 0 us -> 20.8 us
  local copies, waits for them, and re-layouts: 12.6 us -> 22.8 us
  other arithmetic: 16.8 us -> 7.25 us
    ppermute x70 -> x0, waiting for transfers between devices: 559 us -> none  [from_behind(): return lax.ppermute(value, axis, pairs)]
    ppermute x70 -> x0, starting transfers between devices: 143 us -> none  [from_behind(): return lax.ppermute(value, axis, pairs)]
    all_to_all x0 -> x1, blocking collectives: none -> 20.8 us  [on_device(): rebuilt = lax.all_to_all(back, AXES, 0, 0, tiled=True)]
    all_to_all x0 -> x1, starting transfers between devices: none -> 11.9 us  [on_device(): held = lax.all_to_all(sent, AXES, 0, 0, tiled=True)]
    reshape x0 -> x4, local copies, waits for them, and re-layouts: none -> 11.1 us  [the longest x2 6.95 us: on_device(): sent = contrib.reshape(terms, device_count, share).transpose(1, 0, 2)]
  transfers between devices with their start and end apart: 70 -> 1, of which waited for: 70 -> 0; matrix products, arithmetic and copies ran while one was open for 0% -> 1% of each run, Pallas kernels for 0% -> 0%
where the time goes in v1:
time: 104 us; the launch traced here: 103 us
  between operations  37.9 us (36%)
  local copies, waits for them, and re-layouts  22.8 us (22%)
  blocking collectives  20.8 us (20%)
  starting transfers between devices  11.9 us (11%)
  other arithmetic  7.25 us (7%)
  matrix products  1.99 us (2%)
    all_to_all x1, blocking collectives, on_device(): rebuilt = lax.all_to_all(back, AXES, 0, 0, tiled=True)  20.8 us
    all_to_all x1, starting transfers between devices, on_device(): held = lax.all_to_all(sent, AXES, 0, 0, tiled=True)  11.9 us
    reshape x2, local copies, waits for them, and re-layouts, on_device(): sent = contrib.reshape(terms, device_count, share).transpose(1, 0, 2)  6.95 us
    add x2, other arithmetic, on_device(): total = part if total is None else total + part  6.27 us
    unnamed x5, local copies, waits for them, and re-layouts  5.09 us
    reshape x1, local copies, waits for them, and re-layouts, on_device(): sent = sent.reshape(device_count, terms * share // lanes, lanes)  3.38 us
    gather x1, local copies, waits for them, and re-layouts, on_device(): coeffs_used = coefficients[repair_rows, helper_slot]  3.18 us
  transfers between devices with their start and end apart: 1, of which 0 were waited for; matrix products, arithmetic and copies ran while one was open for 1% of the time, Pallas kernels for 0%

profile of v1, /device:TPU:1, one launch (start us, length us, event | category | flops | bytes accessed | tf_op | source)
XLA Modules:
  0.0 102.6 jit_solution(4185015607792525053)
XLA Ops:
  0.0 0.0 copy-start
  0.0 0.8 fusion.25
  0.8 0.1 copy.15
  1.0 0.1 reshape.40
  1.0 0.0 copy-start.1
  1.0 5.1 %copy.16 = bf16[256,10,8,8]{3,2,1,0:T(8,128)(2,1)} copy(bf16[256,10,8,8]{0,3,2,1:T(8,128)(2,1)} %param.6) | data formatting | bytes 655360 | tf_op args[1]
  6.1 3.2 %gather_fusion = bf16[20,8,8]{2,1,0:T(8,128)(2,1)S(1)} fusion(bf16[256,10,8,8]{3,2,1,0:T(8,128)(2,1)} %copy.16, s32[20]{0:T(128)S(1)} %reshape.40), kind=kCustom, calls=%fused_computation | custom fusion | bytes 5280 | tf_op jit(solution)/shard_map/gather | solution.py:22
  9.3 0.0 copy-done.1
  9.3 0.8 gather_fusion.1
  10.2 0.1 gather.13
  10.3 0.1 reshape.54
  10.3 0.0 copy-done
  10.4 0.6 gather_fusion.2
  11.0 2.0 %fusion.27 = f32[2,10,8,4096]{3,2,1,0:T(8,128)} fusion(bf16[2,10,8,8]{3,2,1,0:T(8,128)(2,1)S(1)} %bitcast.44, bf16[2,10,8,4096]{3,2,1,0:T(8,128)(2,1)S(1)} %bitcast.41), kind=kOutput, calls=%fused_computation.83 | convolution fusion | flops 10485760 | bytes 3934720 | tf_op jit(solution)/shard_map/shpq,shql->shpl/dot_general | solution.py:24
  13.0 3.7 %reshape.34 = f32[20,128,256]{2,1,0:T(8,128)} reshape(f32[2,10,8,4096]{3,2,1,0:T(8,128)} %fusion.27) | data formatting | bytes 5242880 | tf_op jit(solution)/shard_map/reshape | solution.py:30
  16.7 3.2 %copy.17 = f32[20,128,256]{1,2,0:T(8,128)} copy(f32[20,128,256]{2,1,0:T(8,128)} %reshape.34) | data formatting | bytes 5242880 | tf_op jit(solution)/shard_map/reshape | solution.py:30
  19.9 3.4 %copy.18 = f32[128,40,128]{2,1,0:T(8,128)} copy(f32[128,40,128]{0,2,1:T(8,128)} %bitcast.40) | data formatting | bytes 5242880 | tf_op jit(solution)/shard_map/reshape | solution.py:31
  23.3 11.9 %all-to-all-start = ((f32[128,40,128]{2,1,0:T(8,128)}), f32[128,40,128]{2,1,0:T(8,128)}, u32[]{:S(2)}, u32[]{:S(2)}) async-start(f32[128,40,128]{2,1,0:T(8,128)} %copy.18), calls=%async_computation | async-start | bytes 5242880 | tf_op jit(solution)/shard_map/all_to_all | solution.py:32
  35.2 0.7 fusion.26
  59.7 0.7 slice.113
  74.4 0.0 all-to-all-done
  74.4 3.1 %add_add_fusion.1 = f32[128,1,2,128]{3,2,1,0:T(2,128)S(1)} fusion(s32[]{:T(128)S(6)} %select_n.100, f32[128,20,2,128]{3,2,1,0:T(2,128)} %bitcast.5, s32[]{:T(128)S(6)} %select_n.99, s32[]{:T(128)S(6)} %select_n.98, s32[]{:T(128)S(6)} %select_n.97, s32[]{:T(128)S(6)} %select_n.96, s32[]{:T(128)S(6)} %select_n.95, s32[]{:T(128)S(6)} %select_n.94, ...), kind=kLoop, calls=%fused_computation.65 | loop fusion | flops 622592 | bytes 2752552 | tf_op jit(solution)/shard_map/add | solution.py:42
  77.5 3.2 %add_add_fusion = f32[128,1,2,128]{3,2,1,0:T(2,128)S(1)} fusion(s32[]{:T(128)S(6)} %select_n.109, f32[128,20,2,128]{3,2,1,0:T(2,128)} %bitcast.5, s32[]{:T(128)S(6)} %select_n.108, s32[]{:T(128)S(6)} %select_n.107, s32[]{:T(128)S(6)} %select_n.106, s32[]{:T(128)S(6)} %select_n.105, s32[]{:T(128)S(6)} %select_n.104, s32[]{:T(128)S(6)} %select_n.103, ...), kind=kLoop, calls=%fused_computation.64 | loop fusion | flops 622592 | bytes 2752552 | tf_op jit(solution)/shard_map/add | solution.py:42
  80.6 0.1 pad_maximum_fusion
  80.8 20.8 %all_to_all.10 = f32[128,4,128]{2,1,0:T(4,128)S(1)} all-to-all(f32[128,4,128]{2,1,0:T(4,128)S(1)} %bitcast.42), channel_id=1, replica_groups=mesh['rack'=4,'node'=32] {'rack','node'}, dimensions={0} | all-to-all | bytes 524288 | tf_op jit(solution)/shard_map/all_to_all | solution.py:45
  101.6 0.1 copy.19
  101.7 0.1 copy.20
  101.9 0.8 reshape.39
  (3 shorter events, 0.0 us)
Async XLA Ops:
  0.0 10.3 %copy-start = (bf16[20,8,4096]{2,1,0:T(8,128)(2,1)S(1)}, bf16[20,8,4096]{2,1,0:T(8,128)(2,1)}, u32[]{:S(2)}) copy-start(bf16[20,8,4096]{2,1,0:T(8,128)(2,1)} %param.5) | copy-start | bytes 3932164
  1.0 8.3 %copy-start.1 = (s32[256,10]{0,1:T(8,128)S(1)}, s32[256,10]{0,1:T(8,128)}, u32[]{:S(2)}) copy-start(s32[256,10]{0,1:T(8,128)} %param.9) | copy-start | bytes 30724
  23.3 51.1 %all-to-all-start = ((f32[128,40,128]{2,1,0:T(8,128)}), f32[128,40,128]{2,1,0:T(8,128)}, u32[]{:S(2)}, u32[]{:S(2)}) async-start(f32[128,40,128]{2,1,0:T(8,128)} %copy.18), calls=%async_computation | async-start | bytes 5242880 | tf_op jit(solution)/shard_map/all_to_all | solution.py:32

commit v2 on v1

v2 whole, which is shorter than its diff:
```python
import jax
import jax.numpy as jnp
from jax import lax
from jax.experimental import pallas as pl
from jax.experimental.pallas import tpu as pltpu
from jax.sharding import PartitionSpec as P

HELPERS = 10
REP_DEV = 2
AXES = ("rack", "node")
LANES = 128
TILE = 8


def offset_of(rack_ref, node_ref, node_count, device_count, s, h):
    return lax.rem(rack_ref[h, s] * node_count + node_ref[h, s], device_count)


def make_terms(node_count, device_count, me_ref, rack_ref, node_ref, slots_ref, coeff_ref, stored_ref,
               out_ref, weight):
    held, planes, columns = stored_ref.shape
    terms = REP_DEV * HELPERS

    @pl.when(pl.program_id(0) == 0)
    def _():
        me = me_ref[0]
        repairs = slots_ref.shape[1]
        width = weight.shape[0] * LANES
        entries = planes * planes
        table = coeff_ref[...].astype(jnp.float32).reshape(HELPERS * entries, repairs).astype(jnp.bfloat16)
        repair = lax.broadcasted_iota(jnp.int32, (HELPERS, repairs), 1)
        own = lax.div(lax.broadcasted_iota(jnp.int32, (HELPERS, HELPERS * entries), 1), entries) == (
            lax.broadcasted_iota(jnp.int32, (HELPERS, HELPERS * entries), 0)
        )
        fold = (
            lax.rem(lax.broadcasted_iota(jnp.int32, (HELPERS * entries, entries), 0), entries)
            == lax.broadcasted_iota(jnp.int32, (HELPERS * entries, entries), 1)
        ).astype(jnp.bfloat16)
        entry = lax.broadcasted_iota(jnp.int32, (entries, width), 0)
        lane = lax.broadcasted_iota(jnp.int32, (entries, width), 1)
        slot_of_lane = lax.div(lax.broadcasted_iota(jnp.int32, (HELPERS, width), 1), planes)
        picked, slots = [], []
        for s in range(REP_DEV):
            offset = lax.rem(rack_ref[:, s : s + 1] * node_count + node_ref[:, s : s + 1], device_count)
            row = lax.rem(me + device_count - offset, device_count) * REP_DEV + s
            chosen = row == repair
            slots.append(jnp.sum(jnp.where(chosen, slots_ref[...], 0), axis=1, keepdims=True))
            every = lax.dot_general(
                chosen.astype(jnp.float32).astype(jnp.bfloat16), table, (((1,), (1,)), ((), ())),
                preferred_element_type=jnp.float32,
            )
            every = jnp.where(own, every, 0.0).astype(jnp.bfloat16)
            picked.append(jnp.dot(every, fold, preferred_element_type=jnp.float32).astype(jnp.bfloat16))
        for p in range(planes):
            spread = (entry == p * planes + lax.rem(lane, planes)).astype(jnp.float32).astype(jnp.bfloat16)
            for s in range(REP_DEV):
                wide = jnp.dot(picked[s], spread, preferred_element_type=jnp.float32)
                wide = jnp.where(slots[s] == slot_of_lane, wide, 0.0)
                first = p * terms + s * HELPERS
                for w in range(weight.shape[0]):
                    weight[w, first : first + HELPERS, :] = wide[:, w * LANES : (w + 1) * LANES]

    blocks = stored_ref[...].astype(jnp.float32).reshape(held * planes, columns).astype(jnp.bfloat16)
    matrix = jnp.concatenate([weight[w] for w in range(weight.shape[0])], 1)[:, : held * planes].astype(jnp.bfloat16)
    result = jnp.dot(matrix, blocks, preferred_element_type=jnp.float32)
    for j in range(columns // LANES):
        out_ref[j] = result[:, j * LANES : (j + 1) * LANES]


def add_terms(node_count, device_count, rack_ref, node_ref, held_hbm, out_ref, held, sems):
    terms = REP_DEV * HELPERS
    per = held_hbm.shape[0] // device_count
    parts = per // terms
    main = pltpu.make_async_copy(held_hbm, held.at[pl.ds(0, device_count * per)], sems.at[0])
    wrap = pltpu.make_async_copy(
        held_hbm.at[pl.ds(0, TILE * per)], held.at[pl.ds(device_count * per, TILE * per)], sems.at[1]
    )
    main.start()
    wrap.start()
    offsets = [offset_of(rack_ref, node_ref, node_count, device_count, k // HELPERS, k % HELPERS) for k in range(terms)]
    main.wait()
    wrap.wait()

    @pl.loop(0, device_count // TILE)
    def _(j):
        starts = [lax.rem(j * TILE + offset, device_count) * per for offset in offsets]
        for s in range(REP_DEV):
            for i in range(parts):
                total = None
                for h in range(HELPERS):
                    k = s * HELPERS + h
                    part = held[pl.ds(starts[k] + (i * terms + k), TILE, stride=per), :]
                    total = part if total is None else total + part
                out_ref[pl.ds(j * TILE * parts * REP_DEV + i * REP_DEV + s, TILE, stride=parts * REP_DEV), :] = total


def place(in_ref, out_ref):
    planes, length = out_ref.shape[1:]
    for s in range(REP_DEV):
        for t in range(length // LANES):
            tile = in_ref[pl.ds(t * planes * REP_DEV + s, planes, stride=REP_DEV), :]
            out_ref[s, :, t * LANES : (t + 1) * LANES] = tile


def on_device(stored, coefficients, helper_rack, helper_node, helper_block):
    node_count = lax.axis_size("node")
    device_count = lax.axis_size(AXES)
    held, planes, length = stored.shape
    terms = REP_DEV * HELPERS
    me = (lax.axis_index("rack") * node_count + lax.axis_index("node")).reshape(1)
    tiles = length // LANES
    step = 4
    racks, nodes, slots = helper_rack.T, helper_node.T, helper_block.T
    table = coefficients.transpose(1, 2, 3, 0)
    index_spec = pl.BlockSpec((HELPERS, LANES), lambda *_: (0, 0), memory_space=pltpu.SMEM)
    sent = pl.pallas_call(
        lambda *refs: make_terms(node_count, device_count, *refs),
        out_shape=jax.ShapeDtypeStruct((tiles, planes * terms, LANES), jnp.float32),
        grid=(tiles // step,),
        in_specs=[
            pl.BlockSpec(memory_space=pltpu.SMEM),
            pl.BlockSpec((HELPERS, LANES), lambda g: (0, 0)),
            pl.BlockSpec((HELPERS, LANES), lambda g: (0, 0)),
            pl.BlockSpec(slots.shape, lambda g: (0, 0)),
            pl.BlockSpec(table.shape, lambda g: (0, 0, 0, 0)),
            pl.BlockSpec((held, planes, step * LANES), lambda g: (0, 0, g)),
        ],
        out_specs=pl.BlockSpec((step, planes * terms, LANES), lambda g: (g, 0, 0)),
        scratch_shapes=[pltpu.VMEM((pl.cdiv(held * planes, LANES), planes * terms, LANES), jnp.float32)],
        name="make_terms",
    )(me, racks, nodes, slots, table, stored)
    per = tiles * planes * terms // device_count
    arrived = lax.all_to_all(sent.reshape(device_count, per, LANES), AXES, 0, 0, tiled=True)
    parts = per // terms
    back = pl.pallas_call(
        lambda *refs: add_terms(node_count, device_count, *refs),
        out_shape=jax.ShapeDtypeStruct((device_count * parts * REP_DEV, LANES), jnp.float32),
        grid=(1,),
        in_specs=[index_spec, index_spec, pl.BlockSpec(memory_space=pl.ANY)],
        out_specs=pl.BlockSpec((device_count * parts * REP_DEV, LANES), lambda g: (0, 0)),
        scratch_shapes=[
            pltpu.VMEM(((device_count + TILE) * per, LANES), jnp.float32),
            pltpu.SemaphoreType.DMA((2,)),
        ],
        name="add_terms",
    )(racks, nodes, arrived.reshape(device_count * per, LANES))
    home = lax.all_to_all(back.reshape(device_count, parts * REP_DEV, LANES), AXES, 0, 0, tiled=True)
    return pl.pallas_call(
        place,
        out_shape=jax.ShapeDtypeStruct((REP_DEV, planes, length), jnp.float32),
        name="place",
    )(home.reshape(device_count * parts * REP_DEV, LANES))


def solution(mesh):
    placed = (P(AXES, None, None), P(), P(), P(), P())
    return jax.shard_map(
        on_device,
        mesh=mesh,
        in_specs=placed,
        out_specs=P(AXES, None, None),
        check_vma=False,
    )
```

time: 104 us -> 78.1 us (0.75)
  blocking collectives: 20.8 us -> 64.4 us
  between operations: 37.9 us -> 0.01 us
  local copies, waits for them, and re-layouts: 22.8 us -> 0 us
  Pallas kernels: 0 us -> 13.3 us
  starting transfers between devices: 11.9 us -> 0 us
  other arithmetic: 7.25 us -> 0 us
  matrix products: 1.99 us -> 0 us
    all_to_all x1 -> x2, blocking collectives: 20.8 us -> 64.4 us  [the longest x1 47.1 us: on_device(): lax.all_to_all(sent.reshape(device_count, per, LANES), AXES, 0, 0, tiled=...]
    pallas_call x0 -> x3, Pallas kernels: none -> 13.3 us  [the longest x1 7.08 us: on_device(): pl.pallas_call(lambda *refs: make_terms(node_count, device_count, *refs),...]
    all_to_all x1 -> x0, starting transfers between devices: 11.9 us -> none  [on_device(): held = lax.all_to_all(sent, AXES, 0, 0, tiled=True)]
    reshape x4 -> x0, local copies, waits for them, and re-layouts: 11.1 us -> none  [the longest x2 6.95 us: on_device(): sent = contrib.reshape(terms, device_count, share).transpose(1, 0, 2)]
    add x2 -> x0, other arithmetic: 6.27 us -> none  [on_device(): total = part if total is None else total + part]
    unnamed x5 -> x0, local copies, waits for them, and re-layouts: 5.09 us -> none
    gather x4 -> x0, local copies, waits for them, and re-layouts: 4.73 us -> none  [the longest x1 3.18 us: on_device(): coeffs_used = coefficients[repair_rows, helper_slot]]
    dot_general x1 -> x0, matrix products: 1.99 us -> none  [on_device(): jnp.einsum('shpq,shql->shpl', coeffs_used, blocks_used, preferred_element...]
  transfers between devices with their start and end apart: 1 -> 0, of which waited for: 0 -> 0; matrix products, arithmetic and copies ran while one was open for 1% -> 0% of each run, Pallas kernels for 0% -> 0%
where the time goes in v2:
time: 78.1 us; the launch traced here: 77.6 us
  blocking collectives  64.4 us (82%)
  Pallas kernels  13.3 us (17%)
    all_to_all x1, blocking collectives, on_device(): lax.all_to_all(sent.reshape(device_count, per, LANES), AXES, 0, 0, tiled=...  47.1 us
    all_to_all x1, blocking collectives, on_device(): lax.all_to_all(back.reshape(device_count, parts * REP_DEV, LANES), AXES,...  17.2 us
    pallas_call x1, Pallas kernels, on_device(): pl.pallas_call(lambda *refs: make_terms(node_count, device_count, *refs),...  7.08 us
    pallas_call x1, Pallas kernels, on_device(): pl.pallas_call(lambda *refs: add_terms(node_count, device_count, *refs),...  4.51 us
    pallas_call x1, Pallas kernels, on_device(): pl.pallas_call(place, out_shape=jax.ShapeDtypeStruct((REP_DEV, planes, le...  1.67 us

profile of v2, /device:TPU:1, one launch (start us, length us, event | category | flops | bytes accessed | tf_op | source)
XLA Modules:
  0.0 77.6 jit_solution(11201387887036677575)
XLA Ops:
  0.0 7.1 %make_terms.1 = f32[32,160,128]{2,1,0:T(8,128)} custom-call(s32[1]{0:T(128)} %bitcast.2.refs_0_, s32[10,256]{1,0:T(8,128)} %bitcast.14, s32[10,256]{1,0:T(8,128)} %bitcast.16, s32[10,256]{1,0:T(8,128)} %bitcast.18, bf16[10,8,8,256]{3,2,1,0:T(8,128)(2,1)} %bitcast.13, bf16[20,8,4096]{2,1,0:T(8,128)(2,1)} %refs_5_.1), custom_call_target="tpu_custom_call" | custom-call | tf_op jit(solution)/shard_map/make_terms/pallas_call | solution.py:116
  7.1 47.1 %all_to_all.10 = f32[128,40,128]{2,1,0:T(8,128)} all-to-all(f32[128,40,128]{2,1,0:T(8,128)} %bitcast.9), channel_id=1, replica_groups=mesh['rack'=4,'node'=32] {'rack','node'}, dimensions={0} | all-to-all | bytes 5242880 | tf_op jit(solution)/shard_map/all_to_all | solution.py:133
  54.2 4.5 %add_terms.1 = f32[512,128]{1,0:T(8,128)} custom-call(s32[10,256]{1,0:T(8,128)} %bitcast.15, s32[10,256]{1,0:T(8,128)} %bitcast.17, f32[5120,128]{1,0:T(8,128)} %bitcast.10), custom_call_target="tpu_custom_call" | custom-call | tf_op jit(solution)/shard_map/add_terms/pallas_call | solution.py:135
  58.7 17.2 %all_to_all.11 = f32[128,4,128]{2,1,0:T(4,128)} all-to-all(f32[128,4,128]{2,1,0:T(4,128)} %bitcast.11), channel_id=1, replica_groups=mesh['rack'=4,'node'=32] {'rack','node'}, dimensions={0} | all-to-all | bytes 524288 | tf_op jit(solution)/shard_map/all_to_all | solution.py:147
  76.0 1.7 %place.1 = f32[2,8,4096]{2,1,0:T(8,128)} custom-call(f32[512,128]{1,0:T(8,128)} %bitcast.12), custom_call_target="tpu_custom_call" | custom-call | tf_op jit(solution)/shard_map/place/pallas_call | solution.py:148

commit v3 on v2

--- a/solution.py
+++ b/solution.py
@@ -112,6 +112,9 @@
     step = 4
     racks, nodes, slots = helper_rack.T, helper_node.T, helper_block.T
     table = coefficients.transpose(1, 2, 3, 0)
+    stored, table, racks, nodes, slots = (
+        pltpu.with_memory_space_constraint(x, pltpu.HBM) for x in (stored, table, racks, nodes, slots)
+    )
     index_spec = pl.BlockSpec((HELPERS, LANES), lambda *_: (0, 0), memory_space=pltpu.SMEM)
     sent = pl.pallas_call(
         lambda *refs: make_terms(node_count, device_count, *refs),
@@ -127,6 +130,7 @@
         ],
         out_specs=pl.BlockSpec((step, planes * terms, LANES), lambda g: (g, 0, 0)),
         scratch_shapes=[pltpu.VMEM((pl.cdiv(held * planes, LANES), planes * terms, LANES), jnp.float32)],
+        compiler_params=pltpu.CompilerParams(vmem_limit_bytes=12 << 20),
         name="make_terms",
     )(me, racks, nodes, slots, table, stored)
     per = tiles * planes * terms // device_count
@@ -142,12 +146,14 @@
             pltpu.VMEM(((device_count + TILE) * per, LANES), jnp.float32),
             pltpu.SemaphoreType.DMA((2,)),
         ],
+        compiler_params=pltpu.CompilerParams(vmem_limit_bytes=12 << 20),
         name="add_terms",
     )(racks, nodes, arrived.reshape(device_count * per, LANES))
     home = lax.all_to_all(back.reshape(device_count, parts * REP_DEV, LANES), AXES, 0, 0, tiled=True)
     return pl.pallas_call(
         place,
         out_shape=jax.ShapeDtypeStruct((REP_DEV, planes, length), jnp.float32),
+        compiler_params=pltpu.CompilerParams(vmem_limit_bytes=4 << 20),
         name="place",
     )(home.reshape(device_count * parts * REP_DEV, LANES))
 

time: 78.1 us -> 71.6 us (0.917)
  Pallas kernels: 13.3 us -> 8.83 us
  blocking collectives: 64.4 us -> 62.5 us
    pallas_call x1, Pallas kernels: 4.51 us -> 2.49 us  [on_device(): pl.pallas_call(lambda *refs: add_terms(node_count, device_count, *refs),...]
    all_to_all x1, blocking collectives: 17.2 us -> 15.6 us  [on_device(): lax.all_to_all(back.reshape(device_count, parts * REP_DEV, LANES), AXES,...]
    pallas_call x1, Pallas kernels: 7.08 us -> 5.62 us  [on_device(): pl.pallas_call(lambda *refs: make_terms(node_count, device_count, *refs),...]
    pallas_call x1, Pallas kernels: 1.67 us -> 0.72 us  [on_device(): pl.pallas_call(place, out_shape=jax.ShapeDtypeStruct((REP_DEV, planes, le...]
where the time goes in v3:
time: 71.6 us; the launch traced here: 71.3 us
  blocking collectives  62.5 us (87%)
  Pallas kernels  8.83 us (12%)
    all_to_all x1, blocking collectives, on_device(): lax.all_to_all(sent.reshape(device_count, per, LANES), AXES, 0, 0, tiled=...  46.8 us
    all_to_all x1, blocking collectives, on_device(): lax.all_to_all(back.reshape(device_count, parts * REP_DEV, LANES), AXES,...  15.6 us
    pallas_call x1, Pallas kernels, on_device(): pl.pallas_call(lambda *refs: make_terms(node_count, device_count, *refs),...  5.62 us
    pallas_call x1, Pallas kernels, on_device(): pl.pallas_call(lambda *refs: add_terms(node_count, device_count, *refs),...  2.49 us

profile of v3, /device:TPU:1, one launch (start us, length us, event | category | flops | bytes accessed | tf_op | source)
XLA Modules:
  0.0 71.3 jit_solution(12584078362204946594)
XLA Ops:
  0.0 5.6 %make_terms.1 = f32[32,160,128]{2,1,0:T(8,128)S(1)} custom-call(s32[1]{0:T(128)} %bitcast.2.refs_0_, s32[10,256]{1,0:T(8,128)} %bitcast.14, s32[10,256]{1,0:T(8,128)} %bitcast.16, s32[10,256]{1,0:T(8,128)} %bitcast.18, bf16[10,8,8,256]{3,2,1,0:T(8,128)(2,1)} %bitcast.13, bf16[20,8,4096]{2,1,0:T(8,128)(2,1)} %refs_5_.1), custom_call_target="tpu_custom_call" | custom-call | tf_op jit(solution)/shard_map/make_terms/pallas_call | solution.py:119
  5.6 46.8 %all_to_all.10 = f32[128,40,128]{2,1,0:T(8,128)S(1)} all-to-all(f32[128,40,128]{2,1,0:T(8,128)S(1)} %bitcast.9), channel_id=1, replica_groups=mesh['rack'=4,'node'=32] {'rack','node'}, dimensions={0} | all-to-all | bytes 5242880 | tf_op jit(solution)/shard_map/all_to_all | solution.py:137
  52.5 2.5 %add_terms.1 = f32[512,128]{1,0:T(8,128)S(1)} custom-call(s32[10,256]{1,0:T(8,128)} %bitcast.15, s32[10,256]{1,0:T(8,128)} %bitcast.17, f32[5120,128]{1,0:T(8,128)S(1)} %bitcast.10), custom_call_target="tpu_custom_call" | custom-call | tf_op jit(solution)/shard_map/add_terms/pallas_call | solution.py:139
  55.0 15.6 %all_to_all.11 = f32[128,4,128]{2,1,0:T(4,128)S(1)} all-to-all(f32[128,4,128]{2,1,0:T(4,128)S(1)} %bitcast.11), channel_id=1, replica_groups=mesh['rack'=4,'node'=32] {'rack','node'}, dimensions={0} | all-to-all | bytes 524288 | tf_op jit(solution)/shard_map/all_to_all | solution.py:152
  70.6 0.7 %place.1 = f32[2,8,4096]{2,1,0:T(8,128)} custom-call(f32[512,128]{1,0:T(8,128)S(1)} %bitcast.12), custom_call_target="tpu_custom_call" | custom-call | tf_op jit(solution)/shard_map/place/pallas_call | solution.py:153

commit v4 on v3

--- a/solution.py
+++ b/solution.py
@@ -109,7 +109,7 @@
     terms = REP_DEV * HELPERS
     me = (lax.axis_index("rack") * node_count + lax.axis_index("node")).reshape(1)
     tiles = length // LANES
-    step = 4
+    step = 16
     racks, nodes, slots = helper_rack.T, helper_node.T, helper_block.T
     table = coefficients.transpose(1, 2, 3, 0)
     stored, table, racks, nodes, slots = (

time: 71.6 us -> 68.5 us (0.957)
  Pallas kernels: 8.83 us -> 5.83 us
    pallas_call x1, Pallas kernels: 5.62 us -> 2.62 us  [on_device(): pl.pallas_call(lambda *refs: make_terms(node_count, device_count, *refs),...]
where the time goes in v4:
time: 68.5 us; the launch traced here: 68.3 us
  blocking collectives  62.5 us (91%)
  Pallas kernels  5.83 us (9%)
    all_to_all x1, blocking collectives, on_device(): lax.all_to_all(sent.reshape(device_count, per, LANES), AXES, 0, 0, tiled=...  46.8 us
    all_to_all x1, blocking collectives, on_device(): lax.all_to_all(back.reshape(device_count, parts * REP_DEV, LANES), AXES,...  15.6 us
    pallas_call x1, Pallas kernels, on_device(): pl.pallas_call(lambda *refs: make_terms(node_count, device_count, *refs),...  2.62 us
    pallas_call x1, Pallas kernels, on_device(): pl.pallas_call(lambda *refs: add_terms(node_count, device_count, *refs),...  2.49 us

profile of v4, /device:TPU:1, one launch (start us, length us, event | category | flops | bytes accessed | tf_op | source)
XLA Modules:
  0.0 68.3 jit_solution(15275212492141229816)
XLA Ops:
  0.0 2.6 %make_terms.1 = f32[32,160,128]{2,1,0:T(8,128)S(1)} custom-call(s32[1]{0:T(128)} %bitcast.2.refs_0_, s32[10,256]{1,0:T(8,128)} %bitcast.14, s32[10,256]{1,0:T(8,128)} %bitcast.16, s32[10,256]{1,0:T(8,128)} %bitcast.18, bf16[10,8,8,256]{3,2,1,0:T(8,128)(2,1)} %bitcast.13, bf16[20,8,4096]{2,1,0:T(8,128)(2,1)} %refs_5_.1), custom_call_target="tpu_custom_call" | custom-call | tf_op jit(solution)/shard_map/make_terms/pallas_call | solution.py:119
  2.6 46.8 %all_to_all.10 = f32[128,40,128]{2,1,0:T(8,128)S(1)} all-to-all(f32[128,40,128]{2,1,0:T(8,128)S(1)} %bitcast.9), channel_id=1, replica_groups=mesh['rack'=4,'node'=32] {'rack','node'}, dimensions={0} | all-to-all | bytes 5242880 | tf_op jit(solution)/shard_map/all_to_all | solution.py:137
  49.4 2.5 %add_terms.1 = f32[512,128]{1,0:T(8,128)S(1)} custom-call(s32[10,256]{1,0:T(8,128)} %bitcast.15, s32[10,256]{1,0:T(8,128)} %bitcast.17, f32[5120,128]{1,0:T(8,128)S(1)} %bitcast.10), custom_call_target="tpu_custom_call" | custom-call | tf_op jit(solution)/shard_map/add_terms/pallas_call | solution.py:139
  52.0 15.6 %all_to_all.11 = f32[128,4,128]{2,1,0:T(4,128)S(1)} all-to-all(f32[128,4,128]{2,1,0:T(4,128)S(1)} %bitcast.11), channel_id=1, replica_groups=mesh['rack'=4,'node'=32] {'rack','node'}, dimensions={0} | all-to-all | bytes 524288 | tf_op jit(solution)/shard_map/all_to_all | solution.py:152
  67.6 0.7 %place.1 = f32[2,8,4096]{2,1,0:T(8,128)} custom-call(f32[512,128]{1,0:T(8,128)S(1)} %bitcast.12), custom_call_target="tpu_custom_call" | custom-call | tf_op jit(solution)/shard_map/place/pallas_call | solution.py:153

commit v5 on v1

v5 whole, which is shorter than its diff:
```python
import jax
import jax.numpy as jnp
from jax import lax
from jax.experimental import pallas as pl
from jax.experimental.pallas import tpu as pltpu
from jax.sharding import PartitionSpec as P

HELPERS = 10
REP_DEV = 2
AXES = ("rack", "node")
LANES = 128
TILE = 8


def offset_of(rack_ref, node_ref, node_count, device_count, s, h):
    return lax.rem(rack_ref[h, s] * node_count + node_ref[h, s], device_count)


def make_terms(node_count, device_count, me_ref, rack_hbm, node_hbm, slots_hbm, coeff_hbm, stored_hbm,
               out_ref, racks, nodes, all_slots, coeffs, blocks, weight, sems):
    chunks, held_planes, columns = blocks.shape
    tiles = columns // LANES
    terms = REP_DEV * HELPERS
    planes = held_planes // terms
    index = [
        pltpu.make_async_copy(source, target, sems.at[n])
        for n, (source, target) in enumerate(
            ((rack_hbm.at[:, pl.ds(0, LANES)], racks), (node_hbm.at[:, pl.ds(0, LANES)], nodes),
             (slots_hbm, all_slots), (coeff_hbm, coeffs))
        )
    ]
    for copy in index:
        copy.start()
    loads = [
        pltpu.make_async_copy(stored_hbm.at[:, pl.ds(c * columns, columns)], blocks.at[c], sems.at[len(index) + c])
        for c in range(chunks)
    ]
    for copy in loads:
        copy.start()
    me = me_ref[0]
    repairs = all_slots.shape[1]
    width = weight.shape[0] * LANES
    entries = planes * planes
    repair = lax.broadcasted_iota(jnp.int32, (HELPERS, repairs), 1)
    own = lax.div(lax.broadcasted_iota(jnp.int32, (HELPERS, HELPERS * entries), 1), entries) == (
        lax.broadcasted_iota(jnp.int32, (HELPERS, HELPERS * entries), 0)
    )
    fold = (
        lax.rem(lax.broadcasted_iota(jnp.int32, (HELPERS * entries, entries), 0), entries)
        == lax.broadcasted_iota(jnp.int32, (HELPERS * entries, entries), 1)
    ).astype(jnp.bfloat16)
    entry = lax.broadcasted_iota(jnp.int32, (entries, width), 0)
    lane = lax.broadcasted_iota(jnp.int32, (entries, width), 1)
    slot_of_lane = lax.div(lax.broadcasted_iota(jnp.int32, (HELPERS, width), 1), planes)
    for copy in index:
        copy.wait()
    table = coeffs[...].astype(jnp.float32).reshape(HELPERS * entries, repairs).astype(jnp.bfloat16)
    picked, slots = [], []
    for s in range(REP_DEV):
        offset = lax.rem(racks[:, s : s + 1] * node_count + nodes[:, s : s + 1], device_count)
        row = lax.rem(me + device_count - offset, device_count) * REP_DEV + s
        chosen = row == repair
        slots.append(jnp.sum(jnp.where(chosen, all_slots[...], 0), axis=1, keepdims=True))
        every = lax.dot_general(
            chosen.astype(jnp.float32).astype(jnp.bfloat16), table, (((1,), (1,)), ((), ())),
            preferred_element_type=jnp.float32,
        )
        every = jnp.where(own, every, 0.0).astype(jnp.bfloat16)
        picked.append(jnp.dot(every, fold, preferred_element_type=jnp.float32).astype(jnp.bfloat16))
    for p in range(planes):
        spread = (entry == p * planes + lax.rem(lane, planes)).astype(jnp.float32).astype(jnp.bfloat16)
        for s in range(REP_DEV):
            wide = jnp.dot(picked[s], spread, preferred_element_type=jnp.float32)
            wide = jnp.where(slots[s] == slot_of_lane, wide, 0.0)
            first = (s * planes + p) * HELPERS
            for w in range(weight.shape[0]):
                weight[w, first : first + HELPERS, :] = wide[:, w * LANES : (w + 1) * LANES]
    matrix = jnp.concatenate([weight[w] for w in range(weight.shape[0])], 1)[:, :held_planes].astype(jnp.bfloat16)
    for c in range(chunks):
        loads[c].wait()
        result = jnp.dot(matrix, blocks[c], preferred_element_type=jnp.float32)
        for j in range(tiles):
            for s in range(REP_DEV):
                out_ref[s, c * tiles + j] = result[s * planes * HELPERS : (s + 1) * planes * HELPERS, j * LANES : (j + 1) * LANES]


def add_terms(node_count, device_count, me_ref, rack_ref, node_ref, held_hbm, out_ref, held, sems):
    per = held_hbm.shape[0] // device_count
    parts = per // HELPERS
    main = pltpu.make_async_copy(held_hbm, held.at[pl.ds(0, device_count * per)], sems.at[0])
    wrap = pltpu.make_async_copy(
        held_hbm.at[pl.ds(0, TILE * per)], held.at[pl.ds(device_count * per, TILE * per)], sems.at[1]
    )
    main.start()
    wrap.start()
    s = lax.div(me_ref[0], device_count // REP_DEV)
    offsets = [lax.rem(rack_ref[h, s] * node_count + node_ref[h, s], device_count) for h in range(HELPERS)]
    main.wait()
    wrap.wait()

    @pl.loop(0, device_count // TILE)
    def _(j):
        starts = [lax.rem(j * TILE + offset, device_count) * per for offset in offsets]
        for i in range(parts):
            total = None
            for h in range(HELPERS):
                part = held[pl.ds(starts[h] + (i * HELPERS + h), TILE, stride=per), :]
                total = part if total is None else total + part
            out_ref[pl.ds(j * TILE * parts + i, TILE, stride=parts), :] = total


def on_device(stored, coefficients, helper_rack, helper_node, helper_block):
    node_count = lax.axis_size("node")
    device_count = lax.axis_size(AXES)
    held, planes, length = stored.shape
    terms = REP_DEV * HELPERS
    me = (lax.axis_index("rack") * node_count + lax.axis_index("node")).reshape(1)
    tiles = length // LANES
    chunks = 2
    racks, nodes, slots = helper_rack.T, helper_node.T, helper_block.T
    table = coefficients.transpose(1, 2, 3, 0)
    blocks = stored.reshape(held * planes, length)
    index_spec = pl.BlockSpec((HELPERS, LANES), lambda *_: (0, 0), memory_space=pltpu.SMEM)
    sent = pl.pallas_call(
        lambda *refs: make_terms(node_count, device_count, *refs),
        out_shape=jax.ShapeDtypeStruct((REP_DEV, tiles, planes * HELPERS, LANES), jnp.float32),
        in_specs=[pl.BlockSpec(memory_space=pltpu.SMEM)] + [pl.BlockSpec(memory_space=pl.ANY)] * 5,
        out_specs=pl.BlockSpec(memory_space=pltpu.VMEM),
        scratch_shapes=[
            pltpu.VMEM((HELPERS, LANES), jnp.int32),
            pltpu.VMEM((HELPERS, LANES), jnp.int32),
            pltpu.VMEM(slots.shape, jnp.int32),
            pltpu.VMEM(table.shape, table.dtype),
            pltpu.VMEM((chunks, held * planes, length // chunks), stored.dtype),
            pltpu.VMEM((pl.cdiv(held * planes, LANES), planes * terms, LANES), jnp.float32),
            pltpu.SemaphoreType.DMA((4 + chunks,)),
        ],
        compiler_params=pltpu.CompilerParams(vmem_limit_bytes=12 << 20),
        name="make_terms",
    )(me, *(pltpu.with_memory_space_constraint(x, pltpu.HBM) for x in (racks, nodes, slots, table, blocks)))
    per = REP_DEV * tiles * planes * HELPERS // device_count
    arrived = lax.all_to_all(sent.reshape(device_count, per, LANES), AXES, 0, 0, tiled=True)
    parts = per // HELPERS
    back = pl.pallas_call(
        lambda *refs: add_terms(node_count, device_count, *refs),
        out_shape=jax.ShapeDtypeStruct((device_count * parts, LANES), jnp.float32),
        grid=(1,),
        in_specs=[pl.BlockSpec(memory_space=pltpu.SMEM), index_spec, index_spec, pl.BlockSpec(memory_space=pl.ANY)],
        out_specs=pl.BlockSpec((device_count * parts, LANES), lambda g: (0, 0)),
        scratch_shapes=[
            pltpu.VMEM(((device_count + TILE) * per, LANES), jnp.float32),
            pltpu.SemaphoreType.DMA((2,)),
        ],
        compiler_params=pltpu.CompilerParams(vmem_limit_bytes=12 << 20),
        name="add_terms",
    )(me, racks, nodes, arrived.reshape(device_count * per, LANES))
    home = lax.all_to_all(back.reshape(device_count, parts, LANES), AXES, 0, 0, tiled=True)
    home = home.reshape(REP_DEV, tiles, planes, LANES).transpose(0, 2, 1, 3)
    return home.reshape(REP_DEV, planes, length)


def solution(mesh):
    placed = (P(AXES, None, None), P(), P(), P(), P())
    return jax.shard_map(
        on_device,
        mesh=mesh,
        in_specs=placed,
        out_specs=P(AXES, None, None),
        check_vma=False,
    )
```

time: 104 us -> 67.9 us (0.65); the launches traced: 103 us -> 67.7 us
  blocking collectives: 20.8 us -> 62.5 us
  between operations: 37.9 us -> 0.03 us
  local copies, waits for them, and re-layouts: 22.8 us -> 0.72 us
  starting transfers between devices: 11.9 us -> 0 us
  other arithmetic: 7.25 us -> 0 us
  Pallas kernels: 0 us -> 4.49 us
  matrix products: 1.99 us -> 0 us
    all_to_all x1 -> x2, blocking collectives: 20.8 us -> 62.5 us  [the longest x1 46.8 us: on_device(): lax.all_to_all(sent.reshape(device_count, per, LANES), AXES, 0, 0, tiled=...]
    all_to_all x1 -> x0, starting transfers between devices: 11.9 us -> none  [on_device(): held = lax.all_to_all(sent, AXES, 0, 0, tiled=True)]
    reshape x4 -> x0, local copies, waits for them, and re-layouts: 11.1 us -> none  [the longest x2 6.95 us: on_device(): sent = contrib.reshape(terms, device_count, share).transpose(1, 0, 2)]
    add x2 -> x0, other arithmetic: 6.27 us -> none  [on_device(): total = part if total is None else total + part]
    gather x4 -> x0, local copies, waits for them, and re-layouts: 4.73 us -> none  [the longest x1 3.18 us: on_device(): coeffs_used = coefficients[repair_rows, helper_slot]]
    pallas_call x0 -> x2, Pallas kernels: none -> 4.49 us  [the longest x1 2.47 us: on_device(): pl.pallas_call(lambda *refs: make_terms(node_count, device_count, *refs),...]
    unnamed x5, local copies, waits for them, and re-layouts: 5.09 us -> 0.72 us
    dot_general x1 -> x0, matrix products: 1.99 us -> none  [on_device(): jnp.einsum('shpq,shql->shpl', coeffs_used, blocks_used, preferred_element...]
  transfers between devices with their start and end apart: 1 -> 0, of which waited for: 0 -> 0; matrix products, arithmetic and copies ran while one was open for 1% -> 0% of each run, Pallas kernels for 0% -> 0%
where the time goes in v5:
time: 67.9 us; the launch traced here: 67.7 us
  blocking collectives  62.5 us (92%)
  Pallas kernels  4.49 us (7%)
  local copies, waits for them, and re-layouts  0.72 us (1%)
    all_to_all x1, blocking collectives, on_device(): lax.all_to_all(sent.reshape(device_count, per, LANES), AXES, 0, 0, tiled=...  46.8 us
    all_to_all x1, blocking collectives, on_device(): lax.all_to_all(back.reshape(device_count, parts, LANES), AXES, 0, 0, tile...  15.6 us
    pallas_call x1, Pallas kernels, on_device(): pl.pallas_call(lambda *refs: make_terms(node_count, device_count, *refs),...  2.47 us
    pallas_call x1, Pallas kernels, on_device(): pl.pallas_call(lambda *refs: add_terms(node_count, device_count, *refs),...  2.01 us

profile of v5, /device:TPU:1, one launch (start us, length us, event | category | flops | bytes accessed | tf_op | source)
XLA Modules:
  0.0 67.7 jit_solution(5115886029380959728)
XLA Ops:
  0.0 2.5 %make_terms.1 = f32[2,32,80,128]{3,2,1,0:T(8,128)S(1)} custom-call(s32[1]{0:T(128)} %bitcast.refs_0_, s32[10,256]{1,0:T(8,128)} %bitcast.17, s32[10,256]{1,0:T(8,128)} %bitcast.19, s32[10,256]{1,0:T(8,128)} %bitcast.24, bf16[10,8,8,256]{3,2,1,0:T(8,128)(2,1)} %bitcast.23, bf16[160,4096]{1,0:T(8,128)(2,1)} %bitcast.21), custom_call_target="tpu_custom_call" | custom-call | tf_op jit(solution)/shard_map/make_terms/pallas_call | solution.py:124
  2.5 0.0 copy-start
  2.5 0.0 copy-start.1
  2.5 46.8 %all_to_all.10 = f32[128,40,128]{2,1,0:T(8,128)S(1)} all-to-all(f32[128,40,128]{2,1,0:T(8,128)S(1)} %bitcast.15), channel_id=1, replica_groups=mesh['rack'=4,'node'=32] {'rack','node'}, dimensions={0} | all-to-all | bytes 5242880 | tf_op jit(solution)/shard_map/all_to_all | solution.py:142
  49.3 0.0 copy-done
  49.3 0.0 copy-done.1
  49.3 2.0 %add_terms.1 = f32[512,128]{1,0:T(8,128)S(1)} custom-call(s32[1]{0:T(128)} %bitcast.refs_0_, s32[10,256]{1,0:T(8,128)S(1)} %bitcast.18, s32[10,256]{1,0:T(8,128)S(1)} %bitcast.20, f32[5120,128]{1,0:T(8,128)S(1)} %bitcast.14), custom_call_target="tpu_custom_call" | custom-call | tf_op jit(solution)/shard_map/add_terms/pallas_call | solution.py:144
  51.4 15.6 %all_to_all.11 = f32[128,4,128]{2,1,0:T(4,128)S(1)} all-to-all(f32[128,4,128]{2,1,0:T(4,128)S(1)} %bitcast.16), channel_id=1, replica_groups=mesh['rack'=4,'node'=32] {'rack','node'}, dimensions={0} | all-to-all | bytes 524288 | tf_op jit(solution)/shard_map/all_to_all | solution.py:157
  67.0 0.7 %copy.7 = f32[2,8,4096]{2,1,0:T(8,128)} copy(f32[2,8,4096]{2,1,0:T(8,128)S(1)} %bitcast.22) | data formatting | bytes 524288
Async XLA Ops:
  2.5 46.9 %copy-start = (s32[256,10]{0,1:T(8,128)S(1)}, s32[256,10]{0,1:T(8,128)}, u32[]{:S(2)}) copy-start(s32[256,10]{0,1:T(8,128)} %param.7) | copy-start | bytes 30724
  2.5 46.8 %copy-start.1 = (s32[256,10]{0,1:T(8,128)S(1)}, s32[256,10]{0,1:T(8,128)}, u32[]{:S(2)}) copy-start(s32[256,10]{0,1:T(8,128)} %param.8) | copy-start | bytes 30724

commit v6 on v5

--- a/solution.py
+++ b/solution.py
@@ -84,17 +84,25 @@
                 out_ref[s, c * tiles + j] = result[s * planes * HELPERS : (s + 1) * planes * HELPERS, j * LANES : (j + 1) * LANES]
 
 
-def add_terms(node_count, device_count, me_ref, rack_ref, node_ref, held_hbm, out_ref, held, sems):
-    per = held_hbm.shape[0] // device_count
+def add_terms(node_count, device_count, me_ref, rack_any, node_any, held_any, out_ref, racks, nodes, held, sems):
+    per = held_any.shape[0] // device_count
     parts = per // HELPERS
-    main = pltpu.make_async_copy(held_hbm, held.at[pl.ds(0, device_count * per)], sems.at[0])
+    index = [
+        pltpu.make_async_copy(source.at[:, pl.ds(0, LANES)], target, sems.at[n])
+        for n, (source, target) in enumerate(((rack_any, racks), (node_any, nodes)))
+    ]
+    main = pltpu.make_async_copy(held_any, held.at[pl.ds(0, device_count * per)], sems.at[2])
     wrap = pltpu.make_async_copy(
-        held_hbm.at[pl.ds(0, TILE * per)], held.at[pl.ds(device_count * per, TILE * per)], sems.at[1]
+        held_any.at[pl.ds(0, TILE * per)], held.at[pl.ds(device_count * per, TILE * per)], sems.at[3]
     )
+    for copy in index:
+        copy.start()
     main.start()
     wrap.start()
+    for copy in index:
+        copy.wait()
     s = lax.div(me_ref[0], device_count // REP_DEV)
-    offsets = [lax.rem(rack_ref[h, s] * node_count + node_ref[h, s], device_count) for h in range(HELPERS)]
+    offsets = [lax.rem(racks[h, s] * node_count + nodes[h, s], device_count) for h in range(HELPERS)]
     main.wait()
     wrap.wait()
 
@@ -116,11 +124,10 @@
     terms = REP_DEV * HELPERS
     me = (lax.axis_index("rack") * node_count + lax.axis_index("node")).reshape(1)
     tiles = length // LANES
-    chunks = 2
+    chunks = 1
     racks, nodes, slots = helper_rack.T, helper_node.T, helper_block.T
     table = coefficients.transpose(1, 2, 3, 0)
     blocks = stored.reshape(held * planes, length)
-    index_spec = pl.BlockSpec((HELPERS, LANES), lambda *_: (0, 0), memory_space=pltpu.SMEM)
     sent = pl.pallas_call(
         lambda *refs: make_terms(node_count, device_count, *refs),
         out_shape=jax.ShapeDtypeStruct((REP_DEV, tiles, planes * HELPERS, LANES), jnp.float32),
@@ -144,12 +151,13 @@
     back = pl.pallas_call(
         lambda *refs: add_terms(node_count, device_count, *refs),
         out_shape=jax.ShapeDtypeStruct((device_count * parts, LANES), jnp.float32),
-        grid=(1,),
-        in_specs=[pl.BlockSpec(memory_space=pltpu.SMEM), index_spec, index_spec, pl.BlockSpec(memory_space=pl.ANY)],
-        out_specs=pl.BlockSpec((device_count * parts, LANES), lambda g: (0, 0)),
+        in_specs=[pl.BlockSpec(memory_space=pltpu.SMEM)] + [pl.BlockSpec(memory_space=pl.ANY)] * 3,
+        out_specs=pl.BlockSpec(memory_space=pltpu.VMEM),
         scratch_shapes=[
+            pltpu.SMEM((HELPERS, LANES), jnp.int32),
+            pltpu.SMEM((HELPERS, LANES), jnp.int32),
             pltpu.VMEM(((device_count + TILE) * per, LANES), jnp.float32),
-            pltpu.SemaphoreType.DMA((2,)),
+            pltpu.SemaphoreType.DMA((4,)),
         ],
         compiler_params=pltpu.CompilerParams(vmem_limit_bytes=12 << 20),
         name="add_terms",

time: 67.9 us -> 67.3 us (level)
  no operation moved by 1% of the time
where the time goes in v6:
time: 67.3 us; the launch traced here: 67.1 us
  blocking collectives  62.5 us (93%)
  Pallas kernels  3.86 us (6%)
  local copies, waits for them, and re-layouts  0.72 us (1%)
    all_to_all x1, blocking collectives, on_device(): lax.all_to_all(sent.reshape(device_count, per, LANES), AXES, 0, 0, tiled=...  46.8 us
    all_to_all x1, blocking collectives, on_device(): lax.all_to_all(back.reshape(device_count, parts, LANES), AXES, 0, 0, tile...  15.6 us
    pallas_call x1, Pallas kernels, on_device(): pl.pallas_call(lambda *refs: make_terms(node_count, device_count, *refs),...  2.32 us
    pallas_call x1, Pallas kernels, on_device(): pl.pallas_call(lambda *refs: add_terms(node_count, device_count, *refs),...  1.54 us

profile of v6, /device:TPU:1, one launch (start us, length us, event | category | flops | bytes accessed | tf_op | source)
XLA Modules:
  0.0 67.1 jit_solution(18081766264834888640)
XLA Ops:
  0.0 2.3 %make_terms.1 = f32[2,32,80,128]{3,2,1,0:T(8,128)S(1)} custom-call(s32[1]{0:T(128)} %bitcast.refs_0_, s32[10,256]{1,0:T(8,128)} %bitcast.17, s32[10,256]{1,0:T(8,128)} %bitcast.19, s32[10,256]{1,0:T(8,128)} %bitcast.24, bf16[10,8,8,256]{3,2,1,0:T(8,128)(2,1)} %bitcast.23, bf16[160,4096]{1,0:T(8,128)(2,1)} %bitcast.21), custom_call_target="tpu_custom_call" | custom-call | tf_op jit(solution)/shard_map/make_terms/pallas_call | solution.py:131
  2.3 0.0 copy-start
  2.3 0.0 copy-start.1
  2.3 46.8 %all_to_all.10 = f32[128,40,128]{2,1,0:T(8,128)S(1)} all-to-all(f32[128,40,128]{2,1,0:T(8,128)S(1)} %bitcast.15), channel_id=1, replica_groups=mesh['rack'=4,'node'=32] {'rack','node'}, dimensions={0} | all-to-all | bytes 5242880 | tf_op jit(solution)/shard_map/all_to_all | solution.py:149
  49.2 0.0 copy-done
  49.2 0.0 copy-done.1
  49.2 1.5 %add_terms.1 = f32[512,128]{1,0:T(8,128)S(1)} custom-call(s32[1]{0:T(128)} %bitcast.refs_0_, s32[10,256]{1,0:T(8,128)S(1)} %bitcast.18, s32[10,256]{1,0:T(8,128)S(1)} %bitcast.20, f32[5120,128]{1,0:T(8,128)S(1)} %bitcast.14), custom_call_target="tpu_custom_call" | custom-call | tf_op jit(solution)/shard_map/add_terms/pallas_call | solution.py:151
  50.7 15.6 %all_to_all.11 = f32[128,4,128]{2,1,0:T(4,128)S(1)} all-to-all(f32[128,4,128]{2,1,0:T(4,128)S(1)} %bitcast.16), channel_id=1, replica_groups=mesh['rack'=4,'node'=32] {'rack','node'}, dimensions={0} | all-to-all | bytes 524288 | tf_op jit(solution)/shard_map/all_to_all | solution.py:165
  66.4 0.7 %copy.7 = f32[2,8,4096]{2,1,0:T(8,128)} copy(f32[2,8,4096]{2,1,0:T(8,128)S(1)} %bitcast.22) | data formatting | bytes 524288
Async XLA Ops:
  2.3 46.9 %copy-start = (s32[256,10]{0,1:T(8,128)S(1)}, s32[256,10]{0,1:T(8,128)}, u32[]{:S(2)}) copy-start(s32[256,10]{0,1:T(8,128)} %param.7) | copy-start | bytes 30724
  2.3 46.8 %copy-start.1 = (s32[256,10]{0,1:T(8,128)S(1)}, s32[256,10]{0,1:T(8,128)}, u32[]{:S(2)}) copy-start(s32[256,10]{0,1:T(8,128)} %param.8) | copy-start | bytes 30724

commit v7 on v6

--- a/solution.py
+++ b/solution.py
@@ -10,6 +10,7 @@
 AXES = ("rack", "node")
 LANES = 128
 TILE = 8
+TURN = 101
 
 
 def offset_of(rack_ref, node_ref, node_count, device_count, s, h):
@@ -101,8 +102,9 @@
     wrap.start()
     for copy in index:
         copy.wait()
-    s = lax.div(me_ref[0], device_count // REP_DEV)
-    offsets = [lax.rem(racks[h, s] * node_count + nodes[h, s], device_count) for h in range(HELPERS)]
+    turn = TURN % device_count
+    s = lax.div(lax.rem(me_ref[0] * turn, device_count), device_count // REP_DEV)
+    offsets = [lax.rem((racks[h, s] * node_count + nodes[h, s]) * turn, device_count) for h in range(HELPERS)]
     main.wait()
     wrap.wait()
 
@@ -115,6 +117,13 @@
                 part = held[pl.ds(starts[h] + (i * HELPERS + h), TILE, stride=per), :]
                 total = part if total is None else total + part
             out_ref[pl.ds(j * TILE * parts + i, TILE, stride=parts), :] = total
+
+
+def ring(count):
+    order = [0] * count
+    for device in range(count):
+        order[device * TURN % count] = device
+    return [order]
 
 
 def on_device(stored, coefficients, helper_rack, helper_node, helper_block):
@@ -146,7 +155,7 @@
         name="make_terms",
     )(me, *(pltpu.with_memory_space_constraint(x, pltpu.HBM) for x in (racks, nodes, slots, table, blocks)))
     per = REP_DEV * tiles * planes * HELPERS // device_count
-    arrived = lax.all_to_all(sent.reshape(device_count, per, LANES), AXES, 0, 0, tiled=True)
+    arrived = lax.all_to_all(sent.reshape(device_count, per, LANES), AXES, 0, 0, tiled=True, axis_index_groups=ring(device_count))
     parts = per // HELPERS
     back = pl.pallas_call(
         lambda *refs: add_terms(node_count, device_count, *refs),
@@ -162,7 +171,7 @@
         compiler_params=pltpu.CompilerParams(vmem_limit_bytes=12 << 20),
         name="add_terms",
     )(me, racks, nodes, arrived.reshape(device_count * per, LANES))
-    home = lax.all_to_all(back.reshape(device_count, parts, LANES), AXES, 0, 0, tiled=True)
+    home = lax.all_to_all(back.reshape(device_count, parts, LANES), AXES, 0, 0, tiled=True, axis_index_groups=ring(device_count))
     home = home.reshape(REP_DEV, tiles, planes, LANES).transpose(0, 2, 1, 3)
     return home.reshape(REP_DEV, planes, length)
 

time: 67.3 us -> 66.2 us (0.984)
  blocking collectives: 62.5 us -> 61.4 us
    all_to_all x1, blocking collectives: 46.8 us -> 45.9 us  [on_device(): lax.all_to_all(sent.reshape(device_count, per, LANES), AXES, 0, 0, tiled=...]
where the time goes in v7:
time: 66.2 us; the launch traced here: 66 us
  blocking collectives  61.4 us (93%)
  Pallas kernels  3.86 us (6%)
  local copies, waits for them, and re-layouts  0.72 us (1%)
    all_to_all x1, blocking collectives, on_device(): lax.all_to_all(sent.reshape(device_count, per, LANES), AXES, 0, 0, tiled=...  45.9 us
    all_to_all x1, blocking collectives, on_device(): lax.all_to_all(back.reshape(device_count, parts, LANES), AXES, 0, 0, tile...  15.5 us
    pallas_call x1, Pallas kernels, on_device(): pl.pallas_call(lambda *refs: make_terms(node_count, device_count, *refs),...  2.32 us
    pallas_call x1, Pallas kernels, on_device(): pl.pallas_call(lambda *refs: add_terms(node_count, device_count, *refs),...  1.55 us

profile of v7, /device:TPU:1, one launch (start us, length us, event | category | flops | bytes accessed | tf_op | source)
XLA Modules:
  0.0 66.0 jit_solution(4579251124506993575)
XLA Ops:
  0.0 2.3 %make_terms.1 = f32[2,32,80,128]{3,2,1,0:T(8,128)S(1)} custom-call(s32[1]{0:T(128)} %bitcast.refs_0_, s32[10,256]{1,0:T(8,128)} %bitcast.17, s32[10,256]{1,0:T(8,128)} %bitcast.19, s32[10,256]{1,0:T(8,128)} %bitcast.24, bf16[10,8,8,256]{3,2,1,0:T(8,128)(2,1)} %bitcast.23, bf16[160,4096]{1,0:T(8,128)(2,1)} %bitcast.21), custom_call_target="tpu_custom_call" | custom-call | tf_op jit(solution)/shard_map/make_terms/pallas_call | solution.py:140
  2.3 0.0 copy-start
  2.3 0.0 copy-start.1
  2.3 45.9 %all_to_all.10 = f32[128,40,128]{2,1,0:T(8,128)S(1)} all-to-all(f32[128,40,128]{2,1,0:T(8,128)S(1)} %bitcast.15), channel_id=1, replica_groups={{0,109,90,71,52,33,14,123,104,85,66,47,28,9,118,99,80,61,42,23,4,113,94..., dimensions={0} | all-to-all | bytes 5242880 | tf_op jit(solution)/shard_map/all_to_all | solution.py:158
  48.2 0.0 copy-done
  48.2 0.0 copy-done.1
  48.2 1.5 %add_terms.1 = f32[512,128]{1,0:T(8,128)S(1)} custom-call(s32[1]{0:T(128)} %bitcast.refs_0_, s32[10,256]{1,0:T(8,128)S(1)} %bitcast.18, s32[10,256]{1,0:T(8,128)S(1)} %bitcast.20, f32[5120,128]{1,0:T(8,128)S(1)} %bitcast.14), custom_call_target="tpu_custom_call" | custom-call | tf_op jit(solution)/shard_map/add_terms/pallas_call | solution.py:160
  49.8 15.5 %all_to_all.11 = f32[128,4,128]{2,1,0:T(4,128)S(1)} all-to-all(f32[128,4,128]{2,1,0:T(4,128)S(1)} %bitcast.16), channel_id=1, replica_groups={{0,109,90,71,52,33,14,123,104,85,66,47,28,9,118,99,80,61,42,23,4,113,94..., dimensions={0} | all-to-all | bytes 524288 | tf_op jit(solution)/shard_map/all_to_all | solution.py:174
  65.3 0.7 %copy.7 = f32[2,8,4096]{2,1,0:T(8,128)} copy(f32[2,8,4096]{2,1,0:T(8,128)S(1)} %bitcast.22) | data formatting | bytes 524288
Async XLA Ops:
  2.3 45.9 %copy-start = (s32[256,10]{0,1:T(8,128)S(1)}, s32[256,10]{0,1:T(8,128)}, u32[]{:S(2)}) copy-start(s32[256,10]{0,1:T(8,128)} %param.7) | copy-start | bytes 30724
  2.3 45.9 %copy-start.1 = (s32[256,10]{0,1:T(8,128)S(1)}, s32[256,10]{0,1:T(8,128)}, u32[]{:S(2)}) copy-start(s32[256,10]{0,1:T(8,128)} %param.8) | copy-start | bytes 30724

commit v8 on v7

--- a/solution.py
+++ b/solution.py
@@ -11,6 +11,7 @@
 LANES = 128
 TILE = 8
 TURN = 101
+PIECES = 1
 
 
 def offset_of(rack_ref, node_ref, node_count, device_count, s, h):
@@ -53,10 +54,13 @@
     entry = lax.broadcasted_iota(jnp.int32, (entries, width), 0)
     lane = lax.broadcasted_iota(jnp.int32, (entries, width), 1)
     slot_of_lane = lax.div(lax.broadcasted_iota(jnp.int32, (HELPERS, width), 1), planes)
+    spreads = [
+        (entry == p * planes + lax.rem(lane, planes)).astype(jnp.float32).astype(jnp.bfloat16) for p in range(planes)
+    ]
     for copy in index:
         copy.wait()
-    table = coeffs[...].astype(jnp.float32).reshape(HELPERS * entries, repairs).astype(jnp.bfloat16)
-    picked, slots = [], []
+    table = coeffs[...].reshape(HELPERS * entries, repairs)
+    every_of, slots = [], []
     for s in range(REP_DEV):
         offset = lax.rem(racks[:, s : s + 1] * node_count + nodes[:, s : s + 1], device_count)
         row = lax.rem(me + device_count - offset, device_count) * REP_DEV + s
@@ -66,12 +70,12 @@
             chosen.astype(jnp.float32).astype(jnp.bfloat16), table, (((1,), (1,)), ((), ())),
             preferred_element_type=jnp.float32,
         )
-        every = jnp.where(own, every, 0.0).astype(jnp.bfloat16)
-        picked.append(jnp.dot(every, fold, preferred_element_type=jnp.float32).astype(jnp.bfloat16))
+        every_of.append(jnp.where(own, every, 0.0).astype(jnp.bfloat16))
+    both = jnp.dot(jnp.concatenate(every_of, 0), fold, preferred_element_type=jnp.float32).astype(jnp.bfloat16)
     for p in range(planes):
-        spread = (entry == p * planes + lax.rem(lane, planes)).astype(jnp.float32).astype(jnp.bfloat16)
+        pair = jnp.dot(both, spreads[p], preferred_element_type=jnp.float32)
         for s in range(REP_DEV):
-            wide = jnp.dot(picked[s], spread, preferred_element_type=jnp.float32)
+            wide = pair[s * HELPERS : (s + 1) * HELPERS]
             wide = jnp.where(slots[s] == slot_of_lane, wide, 0.0)
             first = (s * planes + p) * HELPERS
             for w in range(weight.shape[0]):
@@ -108,7 +112,7 @@
     main.wait()
     wrap.wait()
 
-    @pl.loop(0, device_count // TILE)
+    @pl.loop(0, device_count // TILE, unroll=4)
     def _(j):
         starts = [lax.rem(j * TILE + offset, device_count) * per for offset in offsets]
         for i in range(parts):
@@ -117,6 +121,21 @@
                 part = held[pl.ds(starts[h] + (i * HELPERS + h), TILE, stride=per), :]
                 total = part if total is None else total + part
             out_ref[pl.ds(j * TILE * parts + i, TILE, stride=parts), :] = total
+
+
+def deliver(in_any, out_any, sems):
+    share = in_any.shape[2] // PIECES
+    copies = [
+        pltpu.make_async_copy(
+            in_any.at[s, :, pl.ds(n * share, share)], out_any.at[s, :, pl.ds(n * share, share)], sems.at[s * PIECES + n]
+        )
+        for s in range(REP_DEV)
+        for n in range(PIECES)
+    ]
+    for copy in copies:
+        copy.start()
+    for copy in copies:
+        copy.wait()
 
 
 def ring(count):
@@ -173,7 +192,15 @@
     )(me, racks, nodes, arrived.reshape(device_count * per, LANES))
     home = lax.all_to_all(back.reshape(device_count, parts, LANES), AXES, 0, 0, tiled=True, axis_index_groups=ring(device_count))
     home = home.reshape(REP_DEV, tiles, planes, LANES).transpose(0, 2, 1, 3)
-    return home.reshape(REP_DEV, planes, length)
+    return pl.pallas_call(
+        deliver,
+        out_shape=jax.ShapeDtypeStruct((REP_DEV, planes, length), jnp.float32),
+        in_specs=[pl.BlockSpec(memory_space=pl.ANY)],
+        out_specs=pl.BlockSpec(memory_space=pl.ANY),
+        scratch_shapes=[pltpu.SemaphoreType.DMA((REP_DEV * PIECES,))],
+        compiler_params=pltpu.CompilerParams(vmem_limit_bytes=4 << 20),
+        name="deliver",
+    )(home.reshape(REP_DEV, planes, length))
 
 
 def solution(mesh):

time: 66.2 us -> 66 us (level)
  local copies, waits for them, and re-layouts: 0.72 us -> 0.01 us
    pallas_call x0 -> x1, Pallas kernels: none -> 0.71 us  [on_device(): pl.pallas_call(deliver, out_shape=jax.ShapeDtypeStruct((REP_DEV, planes,...]
    unnamed x5 -> x4, local copies, waits for them, and re-layouts: 0.72 us -> 0.01 us
where the time goes in v8:
time: 66 us; the launch traced here: 65.8 us
  blocking collectives  61.4 us (93%)
  Pallas kernels  4.35 us (7%)
    all_to_all x1, blocking collectives, on_device(): lax.all_to_all(sent.reshape(device_count, per, LANES), AXES, 0, 0, tiled=...  45.9 us
    all_to_all x1, blocking collectives, on_device(): lax.all_to_all(back.reshape(device_count, parts, LANES), AXES, 0, 0, tile...  15.5 us
    pallas_call x1, Pallas kernels, on_device(): pl.pallas_call(lambda *refs: make_terms(node_count, device_count, *refs),...  2.19 us
    pallas_call x1, Pallas kernels, on_device(): pl.pallas_call(lambda *refs: add_terms(node_count, device_count, *refs),...  1.45 us

profile of v8, /device:TPU:1, one launch (start us, length us, event | category | flops | bytes accessed | tf_op | source)
XLA Modules:
  0.0 65.8 jit_solution(18340406990305649448)
XLA Ops:
  0.0 2.2 %make_terms.1 = f32[2,32,80,128]{3,2,1,0:T(8,128)S(1)} custom-call(s32[1]{0:T(128)} %bitcast.refs_0_, s32[10,256]{1,0:T(8,128)} %bitcast.18, s32[10,256]{1,0:T(8,128)} %bitcast.20, s32[10,256]{1,0:T(8,128)} %bitcast.24, bf16[10,8,8,256]{3,2,1,0:T(8,128)(2,1)} %bitcast.23, bf16[160,4096]{1,0:T(8,128)(2,1)} %bitcast.22), custom_call_target="tpu_custom_call" | custom-call | tf_op jit(solution)/shard_map/make_terms/pallas_call | solution.py:159
  2.2 0.0 copy-start
  2.2 0.0 copy-start.1
  2.2 45.9 %all_to_all.10 = f32[128,40,128]{2,1,0:T(8,128)S(1)} all-to-all(f32[128,40,128]{2,1,0:T(8,128)S(1)} %bitcast.15), channel_id=1, replica_groups={{0,109,90,71,52,33,14,123,104,85,66,47,28,9,118,99,80,61,42,23,4,113,94..., dimensions={0} | all-to-all | bytes 5242880 | tf_op jit(solution)/shard_map/all_to_all | solution.py:177
  48.1 0.0 copy-done
  48.1 0.0 copy-done.1
  48.1 1.4 %add_terms.1 = f32[512,128]{1,0:T(8,128)S(1)} custom-call(s32[1]{0:T(128)} %bitcast.refs_0_, s32[10,256]{1,0:T(8,128)S(1)} %bitcast.19, s32[10,256]{1,0:T(8,128)S(1)} %bitcast.21, f32[5120,128]{1,0:T(8,128)S(1)} %bitcast.14), custom_call_target="tpu_custom_call" | custom-call | tf_op jit(solution)/shard_map/add_terms/pallas_call | solution.py:179
  49.6 15.5 %all_to_all.11 = f32[128,4,128]{2,1,0:T(4,128)S(1)} all-to-all(f32[128,4,128]{2,1,0:T(4,128)S(1)} %bitcast.16), channel_id=1, replica_groups={{0,109,90,71,52,33,14,123,104,85,66,47,28,9,118,99,80,61,42,23,4,113,94..., dimensions={0} | all-to-all | bytes 524288 | tf_op jit(solution)/shard_map/all_to_all | solution.py:193
  65.1 0.7 %deliver.1 = f32[2,8,4096]{2,1,0:T(8,128)} custom-call(f32[2,8,4096]{2,1,0:T(8,128)S(1)} %bitcast.17), custom_call_target="tpu_custom_call" | custom-call | tf_op jit(solution)/shard_map/deliver/pallas_call | solution.py:195
Async XLA Ops:
  2.2 45.9 %copy-start = (s32[256,10]{0,1:T(8,128)S(1)}, s32[256,10]{0,1:T(8,128)}, u32[]{:S(2)}) copy-start(s32[256,10]{0,1:T(8,128)} %param.7) | copy-start | bytes 30724
  2.2 45.9 %copy-start.1 = (s32[256,10]{0,1:T(8,128)S(1)}, s32[256,10]{0,1:T(8,128)}, u32[]{:S(2)}) copy-start(s32[256,10]{0,1:T(8,128)} %param.8) | copy-start | bytes 30724

commit v9 on v7

--- a/solution.py
+++ b/solution.py
@@ -26,8 +26,8 @@
     index = [
         pltpu.make_async_copy(source, target, sems.at[n])
         for n, (source, target) in enumerate(
-            ((rack_hbm.at[:, pl.ds(0, LANES)], racks), (node_hbm.at[:, pl.ds(0, LANES)], nodes),
-             (slots_hbm, all_slots), (coeff_hbm, coeffs))
+            ((coeff_hbm, coeffs), (rack_hbm.at[:, pl.ds(0, LANES)], racks),
+             (node_hbm.at[:, pl.ds(0, LANES)], nodes), (slots_hbm, all_slots))
         )
     ]
     for copy in index:
@@ -53,10 +53,13 @@
     entry = lax.broadcasted_iota(jnp.int32, (entries, width), 0)
     lane = lax.broadcasted_iota(jnp.int32, (entries, width), 1)
     slot_of_lane = lax.div(lax.broadcasted_iota(jnp.int32, (HELPERS, width), 1), planes)
+    spreads = [
+        (entry == p * planes + lax.rem(lane, planes)).astype(jnp.float32).astype(jnp.bfloat16) for p in range(planes)
+    ]
     for copy in index:
         copy.wait()
-    table = coeffs[...].astype(jnp.float32).reshape(HELPERS * entries, repairs).astype(jnp.bfloat16)
-    picked, slots = [], []
+    table = coeffs[...].reshape(HELPERS * entries, repairs)
+    every_of, slots = [], []
     for s in range(REP_DEV):
         offset = lax.rem(racks[:, s : s + 1] * node_count + nodes[:, s : s + 1], device_count)
         row = lax.rem(me + device_count - offset, device_count) * REP_DEV + s
@@ -66,12 +69,12 @@
             chosen.astype(jnp.float32).astype(jnp.bfloat16), table, (((1,), (1,)), ((), ())),
             preferred_element_type=jnp.float32,
         )
-        every = jnp.where(own, every, 0.0).astype(jnp.bfloat16)
-        picked.append(jnp.dot(every, fold, preferred_element_type=jnp.float32).astype(jnp.bfloat16))
+        every_of.append(jnp.where(own, every, 0.0).astype(jnp.bfloat16))
+    both = jnp.dot(jnp.concatenate(every_of, 0), fold, preferred_element_type=jnp.float32).astype(jnp.bfloat16)
     for p in range(planes):
-        spread = (entry == p * planes + lax.rem(lane, planes)).astype(jnp.float32).astype(jnp.bfloat16)
+        pair = jnp.dot(both, spreads[p], preferred_element_type=jnp.float32)
         for s in range(REP_DEV):
-            wide = jnp.dot(picked[s], spread, preferred_element_type=jnp.float32)
+            wide = pair[s * HELPERS : (s + 1) * HELPERS]
             wide = jnp.where(slots[s] == slot_of_lane, wide, 0.0)
             first = (s * planes + p) * HELPERS
             for w in range(weight.shape[0]):
@@ -108,7 +111,7 @@
     main.wait()
     wrap.wait()
 
-    @pl.loop(0, device_count // TILE)
+    @pl.loop(0, device_count // TILE, unroll=4)
     def _(j):
         starts = [lax.rem(j * TILE + offset, device_count) * per for offset in offsets]
         for i in range(parts):

time: 66.2 us -> 65.9 us (level)
  no operation moved by 1% of the time
where the time goes in v9:
time: 65.9 us; the launch traced here: 65.7 us
  blocking collectives  61.4 us (93%)
  Pallas kernels  3.56 us (5%)
  local copies, waits for them, and re-layouts  0.72 us (1%)
    all_to_all x1, blocking collectives, on_device(): lax.all_to_all(sent.reshape(device_count, per, LANES), AXES, 0, 0, tiled=...  45.9 us
    all_to_all x1, blocking collectives, on_device(): lax.all_to_all(back.reshape(device_count, parts, LANES), AXES, 0, 0, tile...  15.5 us
    pallas_call x1, Pallas kernels, on_device(): pl.pallas_call(lambda *refs: make_terms(node_count, device_count, *refs),...  2.12 us
    pallas_call x1, Pallas kernels, on_device(): pl.pallas_call(lambda *refs: add_terms(node_count, device_count, *refs),...  1.45 us

profile of v9, /device:TPU:1, one launch (start us, length us, event | category | flops | bytes accessed | tf_op | source)
XLA Modules:
  0.0 65.7 jit_solution(12725050715267278216)
XLA Ops:
  0.0 2.1 %make_terms.1 = f32[2,32,80,128]{3,2,1,0:T(8,128)S(1)} custom-call(s32[1]{0:T(128)} %bitcast.refs_0_, s32[10,256]{1,0:T(8,128)} %bitcast.17, s32[10,256]{1,0:T(8,128)} %bitcast.19, s32[10,256]{1,0:T(8,128)} %bitcast.24, bf16[10,8,8,256]{3,2,1,0:T(8,128)(2,1)} %bitcast.23, bf16[160,4096]{1,0:T(8,128)(2,1)} %bitcast.21), custom_call_target="tpu_custom_call" | custom-call | tf_op jit(solution)/shard_map/make_terms/pallas_call | solution.py:143
  2.1 0.0 copy-start
  2.1 0.0 copy-start.1
  2.1 45.9 %all_to_all.10 = f32[128,40,128]{2,1,0:T(8,128)S(1)} all-to-all(f32[128,40,128]{2,1,0:T(8,128)S(1)} %bitcast.15), channel_id=1, replica_groups={{0,109,90,71,52,33,14,123,104,85,66,47,28,9,118,99,80,61,42,23,4,113,94..., dimensions={0} | all-to-all | bytes 5242880 | tf_op jit(solution)/shard_map/all_to_all | solution.py:161
  48.0 0.0 copy-done
  48.0 0.0 copy-done.1
  48.0 1.4 %add_terms.1 = f32[512,128]{1,0:T(8,128)S(1)} custom-call(s32[1]{0:T(128)} %bitcast.refs_0_, s32[10,256]{1,0:T(8,128)S(1)} %bitcast.18, s32[10,256]{1,0:T(8,128)S(1)} %bitcast.20, f32[5120,128]{1,0:T(8,128)S(1)} %bitcast.14), custom_call_target="tpu_custom_call" | custom-call | tf_op jit(solution)/shard_map/add_terms/pallas_call | solution.py:163
  49.5 15.5 %all_to_all.11 = f32[128,4,128]{2,1,0:T(4,128)S(1)} all-to-all(f32[128,4,128]{2,1,0:T(4,128)S(1)} %bitcast.16), channel_id=1, replica_groups={{0,109,90,71,52,33,14,123,104,85,66,47,28,9,118,99,80,61,42,23,4,113,94..., dimensions={0} | all-to-all | bytes 524288 | tf_op jit(solution)/shard_map/all_to_all | solution.py:177
  65.0 0.7 %copy.7 = f32[2,8,4096]{2,1,0:T(8,128)} copy(f32[2,8,4096]{2,1,0:T(8,128)S(1)} %bitcast.22) | data formatting | bytes 524288
Async XLA Ops:
  2.1 45.9 %copy-start = (s32[256,10]{0,1:T(8,128)S(1)}, s32[256,10]{0,1:T(8,128)}, u32[]{:S(2)}) copy-start(s32[256,10]{0,1:T(8,128)} %param.7) | copy-start | bytes 30724
  2.1 45.9 %copy-start.1 = (s32[256,10]{0,1:T(8,128)S(1)}, s32[256,10]{0,1:T(8,128)}, u32[]{:S(2)}) copy-start(s32[256,10]{0,1:T(8,128)} %param.8) | copy-start | bytes 30724
